TPU v7x, 32 devices: a whole 2x2x4 slice. The times are simulated.
32 devices in a mesh: fsdp: 8 (over z, x), context: 4 (over y, core).
Axes of the slice: x: 2, y: 2, z: 4, core: 2. Of those that a mesh axis runs over, the one named last changes fastest.
Arguments:
- tokens: bfloat16 [16, 1024, 1536], P('fsdp', 'context'), may hold values from -6 to 6
- segments: int32 [16, 1024], P('fsdp', 'context'), may hold values from 0 to 15, never falling along the last dimension, each value on 1 to 512 neighbouring positions
- w_query: bfloat16 [1536, 1536], P('fsdp'), may hold values from -0.15625 to 0.15625
- w_key: bfloat16 [1536, 768], P('fsdp'), may hold values from -0.15625 to 0.15625
- w_value: bfloat16 [1536, 768], P('fsdp'), may hold values from -0.15625 to 0.15625
- w_out: bfloat16 [1536, 1536], P('fsdp'), may hold values from -0.875 to 0.875
- w_gate: bfloat16 [1536, 4096], P('fsdp', 'context'), may hold values from -0.15625 to 0.15625
- w_up: bfloat16 [1536, 4096], P('fsdp', 'context'), may hold values from -0.15625 to 0.15625
- w_down: bfloat16 [4096, 1536], P('context', 'fsdp'), may hold values from -0.09375 to 0.09375
- gain_attn: bfloat16 [1536], P('fsdp'), may hold values from 0.5 to 1.5
- gain_mlp: bfloat16 [1536], P('fsdp'), may hold values from 0.5 to 1.5
- cotangent: bfloat16 [16, 1024, 1536], P('fsdp', 'context'), may hold values from -6 to 6
Outputs:
- output: bfloat16 [16, 1024, 1536], P('fsdp', 'context')
- grad_tokens: float32 [16, 1024, 1536], P('fsdp', 'context')
- grad_w_query: float32 [1536, 1536], P('fsdp')
- grad_w_key: float32 [1536, 768], P('fsdp')
- grad_w_value: float32 [1536, 768], P('fsdp')
- grad_w_out: float32 [1536, 1536], P('fsdp')
- grad_w_gate: float32 [1536, 4096], P('fsdp', 'context')
- grad_w_up: float32 [1536, 4096], P('fsdp', 'context')
- grad_w_down: float32 [4096, 1536], P('context', 'fsdp')
- grad_gain_attn: float32 [1536], P('fsdp')
- grad_gain_mlp: float32 [1536], P('fsdp')
Inputs may be any that keep to these rules, and one draw needn't show every extreme that they name: `segments`: in each sequence segment numbers never fall and all 16 documents appear; the longest has exactly 512 tokens.
All inputs are finite; a program needn't handle non-finite values.
Results may differ from a plain program's by a relative error of at most 0.02.
Values may be sent and summed in bfloat16 or wider, within the bound.
No kernel may reach another device: no remote copies, remote signals or barrier semaphores. Data moves between devices by JAX's collectives and lax.ppermute only.
A program may use at most 256 MiB of HBM per device.

v0:
```python
import functools
import math

import jax
import jax.numpy as jnp
import numpy as np
from jax import lax
from jax.experimental import pallas as pl
from jax.experimental.pallas import tpu as pltpu
from jax.sharding import PartitionSpec as P

H = 16
KVH = 8
HD = 96


EPSILON = 1e-05
THETA = 100000.0


def rms_scale(values, gain):
    return values * lax.rsqrt(jnp.mean(values * values, axis=-1, keepdims=True) + EPSILON) * gain


def rotate(values, cosines, sines):
    half_width = values.shape[-1] // 2
    leading = values[..., :half_width]
    trailing = values[..., half_width:]
    return jnp.concatenate(
        [leading * cosines - trailing * sines, trailing * cosines + leading * sines], axis=-1
    )


def gated(gate_act, up_act):
    return jax.nn.silu(gate_act) * up_act


def inner(left, right):
    return jnp.einsum("ti,tj->ij", left, right, preferred_element_type=jnp.float32)


def outer_back(grad_rows, weight):
    return jnp.einsum("ti,ji->tj", grad_rows, weight, preferred_element_type=jnp.float32)


def reduce_grads(parts):
    shares = (
        lax.psum_scatter(
            parts[0].astype(jnp.bfloat16), "fsdp", scatter_dimension=0, tiled=True
        ).astype(jnp.float32),
        lax.psum_scatter(
            parts[1].astype(jnp.bfloat16), "fsdp", scatter_dimension=0, tiled=True
        ).astype(jnp.float32),
        lax.psum_scatter(
            parts[2].astype(jnp.bfloat16), "fsdp", scatter_dimension=0, tiled=True
        ).astype(jnp.float32),
        lax.psum_scatter(
            parts[3].astype(jnp.bfloat16), "fsdp", scatter_dimension=0, tiled=True
        ).astype(jnp.float32),
        lax.psum_scatter(
            parts[4].astype(jnp.bfloat16), "fsdp", scatter_dimension=0, tiled=True
        ).astype(jnp.float32),
        lax.psum_scatter(
            parts[5].astype(jnp.bfloat16), "fsdp", scatter_dimension=0, tiled=True
        ).astype(jnp.float32),
    )
    result = (
        lax.psum(shares[0].astype(jnp.bfloat16), "context").astype(jnp.float32),
        lax.psum(shares[1].astype(jnp.bfloat16), "context").astype(jnp.float32),
        lax.psum(shares[2].astype(jnp.bfloat16), "context").astype(jnp.float32),
        lax.psum(shares[3].astype(jnp.bfloat16), "context").astype(jnp.float32),
        lax.psum(shares[4].astype(jnp.bfloat16), "context").astype(jnp.float32),
        lax.psum(shares[5].astype(jnp.bfloat16), "context").astype(jnp.float32),
    )
    return result


def gather_attention(shard_query, shard_key, shard_value, shard_out, shard_gain_a, shard_gain_m):
    return (
        lax.all_gather(shard_query, "fsdp", axis=0, tiled=True),
        lax.all_gather(shard_key, "fsdp", axis=0, tiled=True),
        lax.all_gather(shard_value, "fsdp", axis=0, tiled=True),
        lax.all_gather(shard_out, "fsdp", axis=0, tiled=True),
        lax.all_gather(shard_gain_a, "fsdp", axis=0, tiled=True),
        lax.all_gather(shard_gain_m, "fsdp", axis=0, tiled=True),
    )


def gather_mlp(shard_gate, shard_up, shard_down):
    return (
        lax.all_gather(shard_gate, "fsdp", axis=0, tiled=True),
        lax.all_gather(shard_up, "fsdp", axis=0, tiled=True),
        lax.all_gather(shard_down, "fsdp", axis=1, tiled=True),
    )


def on_device_general(
    tokens,
    segments,
    w_query,
    w_key,
    w_value,
    w_out,
    w_gate,
    w_up,
    w_down,
    gain_attn,
    gain_mlp,
    cotangent,
):
    seq_count, tok_local, model_width = tokens.shape
    row_count = seq_count * tok_local
    groups = H // KVH
    kv_width = KVH * HD
    logit_scale = 1.0 / math.sqrt(HD)
    whole_seg = lax.all_gather(segments, "context", axis=1, tiled=True)
    length = whole_seg.shape[1]
    all_rows = seq_count * length
    offset = lax.axis_index("context") * tok_local
    key_index = jnp.arange(length, dtype=jnp.int32)
    query_index = offset + jnp.arange(tok_local, dtype=jnp.int32)
    starts = jnp.concatenate(
        [jnp.ones((seq_count, 1), dtype=bool), whole_seg[:, 1:] != whole_seg[:, :-1]], axis=1
    )
    first_index = lax.cummax(jnp.where(starts, key_index[None, :], 0), axis=1)
    positions = lax.dynamic_slice_in_dim(key_index[None, :] - first_index, offset, tok_local, 1)
    frequency = jnp.power(THETA, -(jnp.arange(HD // 2, dtype=jnp.float32) * 2.0 / HD))
    angles = positions.astype(jnp.float32)[:, :, None] * frequency[None, None, :]
    cosines = jnp.cos(angles).reshape(row_count, 1, HD // 2)
    sines = jnp.sin(angles).reshape(row_count, 1, HD // 2)
    x_flat = tokens.reshape(row_count, model_width).astype(jnp.float32)

    def masked_scores(query_sequence, k_seq, q_seg, k_seg):
        unscaled_scores = (
            jnp.einsum(
                "wxif,axf->xiwa",
                query_sequence,
                k_seq.reshape(length, KVH, HD),
                preferred_element_type=jnp.float32,
            )
            * logit_scale
        )
        allowed = (q_seg[:, None] == k_seg[None, :]) & (key_index[None, :] <= query_index[:, None])
        return jnp.where(allowed[None, None], unscaled_scores, -1e30)

    def attend(items):
        query_sequence, k_seq, v_seq, q_seg, k_seg = items
        scores = masked_scores(query_sequence, k_seq, q_seg, k_seg)
        top_score = jnp.max(scores, axis=-1, keepdims=True)
        weights = jnp.exp(scores - top_score)
        total = jnp.sum(weights, axis=-1, keepdims=True)
        attention_probabilities = (weights / total).astype(jnp.bfloat16)
        mixed_seq = jnp.einsum(
            "uvqe,eua->quva",
            attention_probabilities,
            v_seq.reshape(length, KVH, HD),
            preferred_element_type=jnp.float32,
        ).astype(jnp.bfloat16)
        return (mixed_seq, top_score + jnp.log(total))

    def forward(attn_weights, mlp_weights):
        full_query, full_key, full_value, full_out, full_gain_a, full_gain_m = attn_weights
        normed = rms_scale(x_flat, full_gain_a.astype(jnp.float32)).astype(jnp.bfloat16)
        queries = jnp.dot(normed, full_query, preferred_element_type=jnp.float32).reshape(
            row_count, H, HD
        )
        key_rows = jnp.dot(normed, full_key, preferred_element_type=jnp.float32).reshape(
            row_count, KVH, HD
        )
        value_matrix_rows = jnp.dot(normed, full_value, preferred_element_type=jnp.float32).astype(
            jnp.bfloat16
        )
        qrot = (
            rotate(queries, cosines, sines)
            .astype(jnp.bfloat16)
            .reshape(seq_count, tok_local, KVH, groups, HD)
        )
        rotary_keys = (
            rotate(key_rows, cosines, sines)
            .astype(jnp.bfloat16)
            .reshape(seq_count, tok_local, kv_width)
        )
        all_keys, all_values = (
            lax.all_gather(rotary_keys, "context", axis=1, tiled=True),
            lax.all_gather(
                value_matrix_rows.reshape(seq_count, tok_local, kv_width),
                "context",
                axis=1,
                tiled=True,
            ),
        )
        mixed, log_totals = lax.map(attend, (qrot, all_keys, all_values, segments, whole_seg))
        mixed_flat = mixed.reshape(row_count, H * HD)
        resid = x_flat + jnp.dot(mixed_flat, full_out, preferred_element_type=jnp.float32)
        full_gate, full_up, full_down = mlp_weights
        normed_two = rms_scale(resid, full_gain_m.astype(jnp.float32)).astype(jnp.bfloat16)
        all_normed_two = lax.all_gather(
            normed_two.reshape(seq_count, tok_local, model_width), "context", axis=1, tiled=True
        ).reshape(all_rows, model_width)
        gate_act = jnp.dot(all_normed_two, full_gate, preferred_element_type=jnp.float32)
        up_act = jnp.dot(all_normed_two, full_up, preferred_element_type=jnp.float32)
        hidden = gated(gate_act, up_act).astype(jnp.bfloat16)
        partial_down = jnp.dot(hidden, full_down, preferred_element_type=jnp.float32)
        down_sum = (
            lax.psum_scatter(
                partial_down.reshape(seq_count, length, model_width).astype(jnp.bfloat16),
                "context",
                scatter_dimension=1,
                tiled=True,
            )
            .astype(jnp.float32)
            .reshape(row_count, model_width)
        )
        final = resid + down_sum
        return (
            final,
            normed,
            qrot,
            all_keys,
            all_values,
            mixed,
            log_totals,
            resid,
            all_normed_two,
            gate_act,
            up_act,
            hidden,
        )

    attn_weights = gather_attention(w_query, w_key, w_value, w_out, gain_attn, gain_mlp)
    mlp_weights = gather_mlp(w_gate, w_up, w_down)
    state = forward(attn_weights, mlp_weights)
    output = state[0].astype(jnp.bfloat16).reshape(seq_count, tok_local, model_width)
    (
        final,
        normed,
        qrot,
        all_keys,
        all_values,
        mixed,
        log_totals,
        resid,
        all_normed_two,
        gate_act,
        up_act,
        hidden,
    ) = state
    full_query, full_key, full_value, full_out, full_gain_a, full_gain_m = attn_weights
    full_gate, full_up, full_down = mlp_weights
    grad_out = cotangent.reshape(row_count, model_width)
    all_grad_out = lax.all_gather(cotangent, "context", axis=1, tiled=True).reshape(
        all_rows, model_width
    )
    grad_down_t = inner(all_grad_out, hidden)
    grad_hidden = outer_back(all_grad_out, full_down)
    gate_pull = jax.vjp(gated, gate_act, up_act)[1]
    grad_gate_f, grad_up_f = gate_pull(grad_hidden)
    grad_gate_act = grad_gate_f.astype(jnp.bfloat16)
    grad_up_act = grad_up_f.astype(jnp.bfloat16)
    grad_gate = inner(all_normed_two, grad_gate_act)
    grad_up = inner(all_normed_two, grad_up_act)
    part_normed_two = outer_back(grad_gate_act, full_gate) + outer_back(grad_up_act, full_up)
    grad_normed_two = lax.psum_scatter(
        part_normed_two.reshape(seq_count, length, model_width),
        "context",
        scatter_dimension=1,
        tiled=True,
    ).reshape(row_count, model_width)
    norm_pull = jax.vjp(rms_scale, resid, full_gain_m.astype(jnp.float32))[1]
    back_resid, grad_gain_m = norm_pull(grad_normed_two)
    mlp_shares = (
        lax.psum_scatter(
            grad_gate.astype(jnp.bfloat16), "fsdp", scatter_dimension=0, tiled=True
        ).astype(jnp.float32),
        lax.psum_scatter(
            grad_up.astype(jnp.bfloat16), "fsdp", scatter_dimension=0, tiled=True
        ).astype(jnp.float32),
        lax.psum_scatter(
            grad_down_t.astype(jnp.bfloat16), "fsdp", scatter_dimension=0, tiled=True
        ).astype(jnp.float32),
    )
    grad_resid = grad_out.astype(jnp.float32) + back_resid
    grad_attn = grad_resid.astype(jnp.bfloat16)
    mixed_flat = mixed.reshape(row_count, H * HD)
    grad_out_w = inner(mixed_flat, grad_attn)
    grad_mixed = (
        outer_back(grad_attn, full_out)
        .astype(jnp.bfloat16)
        .reshape(seq_count, tok_local, KVH, groups, HD)
    )

    def attend_back(items):
        query_sequence, k_seq, v_seq, q_seg, k_seg, log_total, grad_seq = items
        scores = masked_scores(query_sequence, k_seq, q_seg, k_seg)
        attention_probabilities = jnp.exp(scores - log_total)
        grad_probs = jnp.einsum(
            "wxif,axf->xiwa",
            grad_seq,
            v_seq.reshape(length, KVH, HD),
            preferred_element_type=jnp.float32,
        )
        weighted = jnp.sum(attention_probabilities * grad_probs, axis=-1, keepdims=True)
        score_gradient = (attention_probabilities * (grad_probs - weighted)).astype(jnp.bfloat16)
        grad_q = (
            jnp.einsum(
                "uvqe,eua->quva",
                score_gradient,
                k_seq.reshape(length, KVH, HD),
                preferred_element_type=jnp.float32,
            )
            * logit_scale
        )
        grad_k = (
            jnp.einsum(
                "jnbp,bjny->pjy", score_gradient, query_sequence, preferred_element_type=jnp.float32
            )
            * logit_scale
        )
        grad_v = jnp.einsum(
            "jnbp,bjny->pjy",
            attention_probabilities.astype(jnp.bfloat16),
            grad_seq,
            preferred_element_type=jnp.float32,
        )
        return (grad_q, grad_k.reshape(length, kv_width), grad_v.reshape(length, kv_width))

    grad_qrot, part_keys, part_values = lax.map(
        attend_back, (qrot, all_keys, all_values, segments, whole_seg, log_totals, grad_mixed)
    )
    grad_krot, grad_vals = (
        lax.psum_scatter(
            part_keys.astype(jnp.bfloat16), "context", scatter_dimension=1, tiled=True
        ).astype(jnp.float32),
        lax.psum_scatter(
            part_values.astype(jnp.bfloat16), "context", scatter_dimension=1, tiled=True
        ).astype(jnp.float32),
    )
    grad_queries = (
        rotate(grad_qrot.reshape(row_count, H, HD), cosines, -sines)
        .astype(jnp.bfloat16)
        .reshape(row_count, H * HD)
    )
    grad_keys = (
        rotate(grad_krot.reshape(row_count, KVH, HD), cosines, -sines)
        .astype(jnp.bfloat16)
        .reshape(row_count, kv_width)
    )
    grad_values = grad_vals.reshape(row_count, kv_width).astype(jnp.bfloat16)
    grad_query_w = inner(normed, grad_queries)
    grad_key_w = inner(normed, grad_keys)
    grad_value_w = inner(normed, grad_values)
    grad_normed = (
        outer_back(grad_queries, full_query)
        + outer_back(grad_keys, full_key)
        + outer_back(grad_values, full_value)
    )
    first_pull = jax.vjp(rms_scale, x_flat, full_gain_a.astype(jnp.float32))[1]
    back_input, grad_gain_a = first_pull(grad_normed)
    attn_grads = reduce_grads(
        (grad_query_w, grad_key_w, grad_value_w, grad_out_w, grad_gain_a, grad_gain_m)
    )
    grad_input = (grad_resid + back_input).reshape(seq_count, tok_local, model_width)
    return (
        output,
        grad_input,
        attn_grads[0],
        attn_grads[1],
        attn_grads[2],
        attn_grads[3],
        mlp_shares[0],
        mlp_shares[1],
        jnp.transpose(mlp_shares[2]),
        attn_grads[4],
        attn_grads[5],
    )


BF = jnp.bfloat16
F32 = jnp.float32
LANES = 128
HALF = HD // 2
NEG = -1e30
SCALE = 1.0 / math.sqrt(HD)
SCALE_LOG2 = SCALE * math.log2(math.e)
CTX = 4
QH = H // CTX
KH = KVH // CTX
BLK = 256
SHARE = 0.25
NT = (((1,), (1,)), ((), ()))
TN = (((0,), (0,)), ((), ()))


def dot_nt(a, b):
    return lax.dot_general(a, b, NT, preferred_element_type=F32)


def dot_tn(a, b):
    return lax.dot_general(a, b, TN, preferred_element_type=F32)


def dot_nn(a, b):
    return jnp.dot(a, b, preferred_element_type=F32)


def lane_iota(rows, width):
    return lax.broadcasted_iota(jnp.int32, (rows, width), 1)


def params(mb, sem):
    return pltpu.CompilerParams(vmem_limit_bytes=mb << 20, dimension_semantics=sem)


def cost(micros):
    return pl.CostEstimate(flops=int(micros * SHARE * 1.15e9), bytes_accessed=0, transcendentals=0)


def packed_columns():
    src = []
    for group in range(6):
        if group < 4:
            member, half = group // 2, group % 2
            for g in range(KH):
                head = 2 * g + member
                src += [head * HD + half * HALF + t for t in range(HALF)]
        else:
            half = group - 4
            for g in range(KH):
                src += [QH * HD + g * HD + half * HALF + t for t in range(HALF)]
        src += [(QH + KH) * HD + group * 32 + t for t in range(32)]
    return np.array(src, np.int32)


def pack_matrix():
    n = (QH + 2 * KH) * HD
    src = jnp.asarray(packed_columns())
    return (lax.broadcasted_iota(jnp.int32, (n, n), 0) == src[None, :]).astype(BF)


def rms_rows(x):
    return x * lax.rsqrt(jnp.mean(x * x, axis=-1, keepdims=True) + EPSILON)


def qkv_kernel(c_ref, x0, x1, x2, x3, w, cos, sin, normed, q, k, v, xs):
    for d, ref in enumerate((x0, x1, x2, x3)):

        @pl.when(pl.program_id(0) == d)
        def _():
            xs[...] = ref[0]

    n = rms_rows(xs[...].astype(F32)).astype(BF)
    normed[...] = n
    t = dot_nn(n, w[...])
    y = [t[:, LANES * p : LANES * (p + 1)] for p in range(6)]
    c, s = cos[...], sin[...]
    rot = []
    for p in range(0, 6, 2):
        rot += [y[p] * c - y[p + 1] * s, y[p + 1] * c + y[p] * s]
    for p in range(4):
        q[:, LANES * p : LANES * (p + 1)] = rot[p].astype(BF)
    for p in range(2):
        k[:, LANES * p : LANES * (p + 1)] = rot[4 + p].astype(BF)
    quarter = lane_iota(y[0].shape[0], LANES) // 32

    def place(parts):
        out = jnp.ones_like(y[0])
        for dst, p in parts:
            piece = y[p] if dst == 3 else pltpu.roll(y[p], 32 * (dst + 1), 1)
            out = jnp.where(quarter == dst, piece, out)
        return out.astype(BF)

    v[:, 0:128] = place(((0, 0), (1, 1), (2, 2), (3, 0)))
    v[:, 128:256] = place(((0, 1), (1, 2)))
    v[:, 256:384] = place(((2, 3), (3, 4)))
    v[:, 384:512] = place(((0, 5), (1, 3), (2, 4), (3, 5)))


def qkv_call(c, xs, w, cos, sin):
    seqs, tok, width = xs[0].shape
    total = seqs * CTX * tok
    cols = 768

    def own(d):
        return pl.BlockSpec(
            (1, tok, width),
            lambda i, s, c: (jnp.where(i == d, s, jnp.where(i < d, 0, seqs - 1)), 0, 0),
        )

    def rows(n):
        return pl.BlockSpec((tok, n), lambda i, s, c: (s * CTX + (i ^ c[0]), 0))

    return pl.pallas_call(
        qkv_kernel,
        grid_spec=pltpu.PrefetchScalarGridSpec(
            num_scalar_prefetch=1,
            grid=(CTX, seqs),
            in_specs=[
                own(0),
                own(1),
                own(2),
                own(3),
                pl.BlockSpec((width, cols), lambda i, s, c: (0, 0)),
                rows(LANES),
                rows(LANES),
            ],
            out_specs=[rows(width), rows(512), rows(256), rows(512)],
            scratch_shapes=[pltpu.VMEM((tok, width), BF)],
        ),
        out_shape=[
            jax.ShapeDtypeStruct((total, width), BF),
            jax.ShapeDtypeStruct((total, 512), BF),
            jax.ShapeDtypeStruct((total, 256), BF),
            jax.ShapeDtypeStruct((total, 512), BF),
        ],
        compiler_params=params(40, ("arbitrary", "arbitrary")),
        cost_estimate=cost(13),
        name="qkv",
    )(c, *xs, w, cos, sin)


def head_masks(rows):
    lane = lane_iota(rows, 256)
    inner_lane = lane % LANES
    by_kv = [inner_lane < HALF, (inner_lane >= HALF) & (inner_lane < HD)]
    in_mixed = [
        lane < HD,
        (lane >= HD) & (lane < 2 * HD),
        (lane >= 64) & (lane < 64 + HD),
        lane >= 64 + HD,
    ]
    return lane, by_kv, in_mixed


def attend_kernel(js_ref, c_ref, q, k, v, start, mixed, lse, vt_s, m_s, o_s):
    s_id, i = pl.program_id(0), pl.program_id(1)
    blocks = k.shape[0] // BLK
    lane, by_kv, in_mixed = head_masks(BLK)
    sub = lax.broadcasted_iota(jnp.int32, (256, BLK), 0)
    take_a = (sub < HD) | ((sub >= 192) & (sub < 224))
    take_b = ((sub >= 64) & (sub < 64 + HD)) | (sub < 32)
    zero = jnp.zeros((BLK, 256), BF)

    @pl.when(i == 0)
    def _():
        for b in range(blocks):
            vt_s[b] = jnp.transpose(v[b * BLK : (b + 1) * BLK, :])

    m_s[...] = jnp.full_like(m_s, -jnp.inf)
    o_s[...] = jnp.zeros_like(o_s)
    col = i * BLK + lax.broadcasted_iota(jnp.int32, (BLK, BLK), 1)
    first = start[0, 0]
    low = js_ref[s_id * CTX + i]

    def step(t, _):
        j = i - t
        kb = k[pl.ds(pl.multiple_of(j * BLK, BLK), BLK), :]
        row = j * BLK + lax.broadcasted_iota(jnp.int32, (BLK, BLK), 0)
        bias = jnp.where((row >= first) & (row <= col), 0.0, NEG)
        for win, take in enumerate((take_a, take_b)):
            vt = vt_s[j, 256 * win : 256 * (win + 1), :]
            outs, alphas = [], []
            for m in range(2):
                h = 2 * win + m
                qh = jnp.where(by_kv[win], q[:, 256 * m : 256 * (m + 1)], zero)
                sc = dot_nt(kb, qh) * SCALE_LOG2 + bias
                m_old = m_s[h : h + 1, :]
                m_new = jnp.maximum(m_old, jnp.max(sc, axis=0, keepdims=True))
                p = jnp.exp2(sc - m_new)
                alphas.append(jnp.exp2(m_old - m_new))
                m_s[h : h + 1, :] = m_new
                outs.append(dot_nn(vt, p.astype(BF)))
            o_s[win] = o_s[win] * jnp.where(take, alphas[0], alphas[1]) + jnp.where(take, outs[0], outs[1])
        return 0

    lax.fori_loop(0, i - low + 1, step, 0)
    sums = [o_s[0, 192:193, :], o_s[0, 224:225, :], o_s[1, 0:1, :], o_s[1, 32:33, :]]
    inv = [1.0 / x for x in sums]
    a = jnp.transpose(o_s[0] * jnp.where(take_a, inv[0], inv[1]))
    b = jnp.transpose(o_s[1] * jnp.where(take_b, inv[2], inv[3]))
    mixed[0, 0, :, 0:128] = a[:, 0:128].astype(BF)
    mixed[0, 0, :, 128:256] = jnp.where(lane[:, :LANES] < 64, a[:, 128:256], b[:, 0:128]).astype(BF)
    mixed[0, 0, :, 256:384] = b[:, 128:256].astype(BF)
    lse[0, 0] = jnp.zeros_like(lse[0, 0])
    for h in range(QH):
        lse[0, 0, h : h + 1, :] = m_s[h : h + 1, :] + jnp.log2(sums[h])


def attend_call(c, js, q, k, v, start, seqs, length):
    blocks = length // BLK
    return pl.pallas_call(
        attend_kernel,
        grid_spec=pltpu.PrefetchScalarGridSpec(
            num_scalar_prefetch=2,
            grid=(seqs, blocks),
            in_specs=[
                pl.BlockSpec((BLK, 512), lambda s, i, js, c: (s * CTX + i, 0)),
                pl.BlockSpec((length, 256), lambda s, i, js, c: (s, 0)),
                pl.BlockSpec((length, 512), lambda s, i, js, c: (s, 0)),
                pl.BlockSpec((1, 1, 1, BLK), lambda s, i, js, c: (s, i, 0, 0)),
            ],
            out_specs=[
                pl.BlockSpec((1, 1, BLK, QH * HD), lambda s, i, js, c: (i ^ c[0], s, 0, 0)),
                pl.BlockSpec((1, 1, 8, BLK), lambda s, i, js, c: (s, i, 0, 0)),
            ],
            scratch_shapes=[
                pltpu.VMEM((blocks, 512, BLK), BF),
                pltpu.VMEM((8, BLK), F32),
                pltpu.VMEM((2, 256, BLK), F32),
            ],
        ),
        out_shape=[
            jax.ShapeDtypeStruct((CTX, seqs, BLK, QH * HD), BF),
            jax.ShapeDtypeStruct((seqs, blocks, 8, BLK), F32),
        ],
        compiler_params=params(40, ("arbitrary", "arbitrary")),
        cost_estimate=cost(18),
        name="attend",
    )(js, c, q, k, v, start)


def attend_back_kernel(
    js_ref, c_ref, q, k, v, o, d0, d1, d23, lse, start, cos, sin, out, do_s, dl_s, kt_s, dq_s, dk_s, dv_s
):
    s_id = pl.program_id(0)
    c = c_ref[0]
    blocks = q.shape[0] // BLK
    lane, by_kv, in_mixed = head_masks(BLK)
    zero = jnp.zeros((BLK, 256), BF)
    mixed_lane = lane_iota(8, QH * HD)
    mixed_row = lax.broadcasted_iota(jnp.int32, (8, QH * HD), 0)
    picks = (mixed_lane // HD == mixed_row).astype(F32)
    for d in range(CTX):
        b = d ^ c
        rows = pl.ds(pl.multiple_of(b * BLK, BLK), BLK)
        g = d0[0, 0] if d == 0 else d1[0] if d == 1 else d23[d - 2, 0]
        do_s[rows, :] = g
        prod = g.astype(F32) * o[d, 0].astype(F32)
        dl_s[b] = lax.dot_general(
            picks, prod, NT, preferred_element_type=F32, precision=lax.Precision.HIGHEST
        )
    for b in range(blocks):
        kt_s[b] = jnp.transpose(k[b * BLK : (b + 1) * BLK, :])
    sub_in = lax.broadcasted_iota(jnp.int32, (256, BLK), 0) % LANES
    sub_kv = [sub_in < HALF, (sub_in >= HALF) & (sub_in < HD)]
    dq_s[...] = jnp.zeros_like(dq_s)
    dk_s[...] = jnp.zeros_like(dk_s)
    dv_s[...] = jnp.zeros_like(dv_s)

    def outer(i, _):
        qs = pl.ds(pl.multiple_of(i * BLK, BLK), BLK)
        col = i * BLK + lax.broadcasted_iota(jnp.int32, (BLK, BLK), 1)
        first = start[0, i]
        delta = dl_s[i]
        logs = lse[0, i]

        def step(t, _):
            j = i - t
            ks = pl.ds(pl.multiple_of(j * BLK, BLK), BLK)
            kb = k[ks, :]
            kt = kt_s[j]
            row = j * BLK + lax.broadcasted_iota(jnp.int32, (BLK, BLK), 0)
            bias = jnp.where((row >= first) & (row <= col), 0.0, NEG)
            dk = jnp.zeros((BLK, 256), F32)
            dq = [jnp.zeros((256, BLK), F32) for _ in range(2)]
            for win in range(KH):
                vb = v[ks, 256 * win : 256 * (win + 1)]
                kg = jnp.where(sub_kv[win], kt, zero)
                dv = jnp.zeros((BLK, 256), F32)
                for m in range(2):
                    h = 2 * win + m
                    qh = jnp.where(by_kv[win], q[qs, 256 * m : 256 * (m + 1)], zero)
                    do = jnp.where(in_mixed[h], do_s[qs, LANES * win : LANES * win + 256], zero)
                    sc = dot_nt(kb, qh) * SCALE_LOG2 + bias
                    p = jnp.exp2(sc - logs[h : h + 1, :])
                    dp = dot_nt(vb, do)
                    ds = (p * (dp - delta[h : h + 1, :])).astype(BF)
                    dv = dv + dot_nn(p.astype(BF), do)
                    dk = dk + dot_nn(ds, qh)
                    dq[m] = dq[m] + dot_nn(kg, ds)
                dv_s[ks, 256 * win : 256 * (win + 1)] += dv
            dk_s[ks, :] += dk
            for m in range(2):
                dq_s[i, m] += dq[m]
            return 0

        lax.fori_loop(0, i - js_ref[s_id * CTX + i] + 1, step, 0)
        return 0

    lax.fori_loop(0, blocks, outer, 0)
    head_lane = lane[:, :LANES] < HD

    def finish(i, _):
        rows = pl.ds(pl.multiple_of(i * BLK, BLK), BLK)
        cs, sn = cos[rows, :] * SCALE, sin[rows, :] * SCALE
        a0, a1 = dv_s[rows, 0:128], dv_s[rows, 128:256]
        b0, b1 = dv_s[rows, 256:384], dv_s[rows, 384:512]

        def r(x, n):
            return pltpu.roll(x, n, 1)

        pieces = [
            r(a0, 96) + a0,
            r(a0, 64) + r(a1, 96),
            r(a0, 32) + r(a1, 64),
            r(b0, 32) + r(b1, 64),
            b0 + r(b1, 32),
            r(b1, 96) + b1,
        ]
        grads = []
        for m in range(2):
            dq = jnp.transpose(dq_s[i, m])
            grads += [dq[:, 0:128], dq[:, 128:256]]
        grads += [dk_s[rows, 0:128], dk_s[rows, 128:256]]
        for p in range(0, 6, 2):
            first_half = grads[p] * cs + grads[p + 1] * sn
            second_half = grads[p + 1] * cs - grads[p] * sn
            out[rows, LANES * p : LANES * (p + 1)] = jnp.where(head_lane, first_half, pieces[p]).astype(BF)
            out[rows, LANES * (p + 1) : LANES * (p + 2)] = jnp.where(
                head_lane, second_half, pieces[p + 1]
            ).astype(BF)
        return 0

    lax.fori_loop(0, blocks, finish, 0)


def attend_back_call(c, js, q, k, v, o, d0, d1, d23, lse, start, cos, sin, seqs, length):
    blocks = length // BLK
    width = QH * HD
    return pl.pallas_call(
        attend_back_kernel,
        grid_spec=pltpu.PrefetchScalarGridSpec(
            num_scalar_prefetch=2,
            grid=(seqs,),
            in_specs=[
                pl.BlockSpec((length, 512), lambda s, js, c: (s, 0)),
                pl.BlockSpec((length, 256), lambda s, js, c: (s, 0)),
                pl.BlockSpec((length, 512), lambda s, js, c: (s, 0)),
                pl.BlockSpec((CTX, 1, BLK, width), lambda s, js, c: (0, s, 0, 0)),
                pl.BlockSpec((1, 1, BLK, width), lambda s, js, c: (0, s, 0, 0)),
                pl.BlockSpec((1, BLK, width), lambda s, js, c: (s, 0, 0)),
                pl.BlockSpec((2, 1, BLK, width), lambda s, js, c: (0, s, 0, 0)),
                pl.BlockSpec((1, blocks, 8, BLK), lambda s, js, c: (s, 0, 0, 0)),
                pl.BlockSpec((1, blocks, 1, BLK), lambda s, js, c: (s, 0, 0, 0)),
                pl.BlockSpec((length, LANES), lambda s, js, c: (s, 0)),
                pl.BlockSpec((length, LANES), lambda s, js, c: (s, 0)),
            ],
            out_specs=pl.BlockSpec((length, 768), lambda s, js, c: (s, 0)),
            scratch_shapes=[
                pltpu.VMEM((length, width), BF),
                pltpu.VMEM((blocks, 8, BLK), F32),
                pltpu.VMEM((blocks, 256, BLK), BF),
                pltpu.VMEM((blocks, 2, 256, BLK), F32),
                pltpu.VMEM((length, 256), F32),
                pltpu.VMEM((length, 512), F32),
            ],
        ),
        out_shape=jax.ShapeDtypeStruct((seqs * length, 768), BF),
        compiler_params=params(48, ("arbitrary",)),
        cost_estimate=cost(31),
        name="attend_back",
    )(js, c, q, k, v, o, d0, d1, d23, lse, start, cos, sin)


def assemble_kernel(c_ref, f_ref, p0, p1, p2, p3, out):
    quarter = p0.shape[-1]
    for b in range(CTX):
        for d, ref in enumerate((p0, p1, p2, p3)):

            @pl.when((b ^ c_ref[0]) == d)
            def _():
                out[:, b * quarter : (b + 1) * quarter] = ref[0]


def assemble_call(c, f, parts):
    count, rows, quarter = parts[0].shape
    part = pl.BlockSpec((1, rows, quarter), lambda b, c, f: (b ^ f[0], 0, 0))
    return pl.pallas_call(
        assemble_kernel,
        grid_spec=pltpu.PrefetchScalarGridSpec(
            num_scalar_prefetch=2,
            grid=(count,),
            in_specs=[part] * CTX,
            out_specs=pl.BlockSpec((rows, CTX * quarter), lambda b, c, f: (b, 0)),
        ),
        out_shape=jax.ShapeDtypeStruct((count * rows, CTX * quarter), BF),
        compiler_params=params(20, ("arbitrary",)),
        cost_estimate=cost(5),
        name="assemble",
    )(c, f, *parts)


def out_kernel(c_ref, x, m0, m1, m2, m3, w, resid, normed):
    c = c_ref[0]
    acc = x[0].astype(F32)
    for d, ref in enumerate((m0, m1, m2, m3)):
        rows = pl.ds(pl.multiple_of((d ^ c) * (QH * HD), QH * HD), QH * HD)
        acc = acc + dot_nn(ref[0, 0], w[rows, :])
    resid[0] = acc
    normed[0] = rms_rows(acc).astype(BF)


def out_call(c, x, mixed, r1, r2, w):
    seqs, tok, width = x.shape
    inner_w = QH * HD

    def slot(n):
        return pl.BlockSpec((1, 1, tok, inner_w), lambda s, c: (n, s, 0, 0))

    tile = pl.BlockSpec((1, tok, width), lambda s, c: (s, 0, 0))
    return pl.pallas_call(
        out_kernel,
        grid_spec=pltpu.PrefetchScalarGridSpec(
            num_scalar_prefetch=1,
            grid=(seqs,),
            in_specs=[
                tile,
                slot(0),
                slot(0),
                slot(0),
                slot(1),
                pl.BlockSpec((H * HD, width), lambda s, c: (0, 0)),
            ],
            out_specs=[tile, tile],
        ),
        out_shape=[
            jax.ShapeDtypeStruct((seqs, tok, width), F32),
            jax.ShapeDtypeStruct((seqs, tok, width), BF),
        ],
        compiler_params=params(48, ("arbitrary",)),
        cost_estimate=cost(8),
        name="out_proj",
    )(c, x, mixed, r1, r2, r2, w)


def rms_back(v, dyg):
    r = lax.rsqrt(jnp.mean(v * v, axis=-1, keepdims=True) + EPSILON)
    return r * dyg - v * (r * r * r * jnp.mean(dyg * v, axis=-1, keepdims=True))


def out_back_kernel(c_ref, part_a, part_b, resid, dy, w, dresid, dattn, dmixed):
    c = c_ref[0]
    dn = part_a[0].astype(F32) + part_b[0].astype(F32)
    total = dy[0].astype(F32) + rms_back(resid[0], dn)
    dresid[0] = total
    low = total.astype(BF)
    dattn[0] = low
    for d in range(CTX):
        rows = pl.ds(pl.multiple_of((d ^ c) * (QH * HD), QH * HD), QH * HD)
        dmixed[d, 0] = dot_nt(low, w[rows, :]).astype(BF)


def out_back_call(c, part_a, part_b, resid, dy, w):
    seqs, tok, width = dy.shape
    inner_w = QH * HD
    tile = pl.BlockSpec((1, tok, width), lambda s, c: (s, 0, 0))
    return pl.pallas_call(
        out_back_kernel,
        grid_spec=pltpu.PrefetchScalarGridSpec(
            num_scalar_prefetch=1,
            grid=(seqs,),
            in_specs=[
                tile,
                tile,
                tile,
                tile,
                pl.BlockSpec((H * HD, width), lambda s, c: (0, 0)),
            ],
            out_specs=[
                tile,
                tile,
                pl.BlockSpec((CTX, 1, tok, inner_w), lambda s, c: (0, s, 0, 0)),
            ],
        ),
        out_shape=[
            jax.ShapeDtypeStruct((seqs, tok, width), F32),
            jax.ShapeDtypeStruct((seqs, tok, width), BF),
            jax.ShapeDtypeStruct((CTX, seqs, tok, inner_w), BF),
        ],
        compiler_params=params(56, ("arbitrary",)),
        cost_estimate=cost(9.5),
        name="out_back",
    )(c, part_a, part_b, resid, dy, w)


def mlp_kernel(n2, dy, wg, wu, wd, hidden, grads):
    n, g_out = n2[...], dy[...]
    gate = dot_nn(n, wg[...])
    up = dot_nn(n, wu[...])
    dh = dot_nn(g_out, wd[...])
    sig = 1.0 / (1.0 + jnp.exp(-gate))
    act = gate * sig
    hidden[...] = (act * up).astype(BF)
    cols = wg.shape[1]
    grads[0] = (dh * up * (sig + act * (1.0 - sig))).astype(BF)
    grads[1] = (dh * act).astype(BF)


def mlp_call(n2, dy, w):
    rows, width = n2.shape
    ff = w.shape[1] // 3
    tile = BLK
    steps = ff // tile
    full = pl.BlockSpec((rows, width), lambda j: (0, 0))
    return pl.pallas_call(
        mlp_kernel,
        grid=(steps,),
        in_specs=[
            full,
            full,
            pl.BlockSpec((width, tile), lambda j: (0, j)),
            pl.BlockSpec((width, tile), lambda j: (0, j + steps)),
            pl.BlockSpec((width, tile), lambda j: (0, j + 2 * steps)),
        ],
        out_specs=[
            pl.BlockSpec((rows, tile), lambda j: (0, j)),
            pl.BlockSpec((2, rows, tile), lambda j: (0, 0, j)),
        ],
        out_shape=[
            jax.ShapeDtypeStruct((rows, ff), BF),
            jax.ShapeDtypeStruct((2, rows, ff), BF),
        ],
        compiler_params=params(40, ("arbitrary",)),
        cost_estimate=cost(4.5),
        name="mlp",
    )(n2, dy, w, w, w)


def sum_nt_kernel(slots, *refs):
    count = len(slots)
    out = refs[-1]
    acc = None
    for n in range(count):
        left = refs[n]
        part = dot_nt(left[0] if len(left.shape) == 3 else left[...], refs[count + n][...])
        acc = part if acc is None else acc + part
    out[...] = acc.astype(out.dtype)


def sum_nt_call(terms, tile):
    rows, k = terms[0][0].shape[-2:]
    n = terms[0][2].shape[0]
    lefts, rights = [], []
    for array, slot, weight, window in terms:
        if slot is None:
            lefts.append(pl.BlockSpec((rows, k), lambda j: (0, 0)))
        else:
            lefts.append(pl.BlockSpec((1, rows, k), functools.partial(lambda slot, j: (slot, 0, 0), slot)))
        rights.append(pl.BlockSpec((tile, k), functools.partial(lambda window, j: (j, window), window)))
    count = len(terms)
    return pl.pallas_call(
        functools.partial(sum_nt_kernel, tuple(t[1] for t in terms)),
        grid=(n // tile,),
        in_specs=lefts + rights,
        out_specs=pl.BlockSpec((rows, tile), lambda j: (0, j)),
        out_shape=jax.ShapeDtypeStruct((rows, n), BF),
        compiler_params=params(40, ("arbitrary",)),
        cost_estimate=cost(4.4),
        name="sum_nt",
    )(*[t[0] for t in terms], *[t[2] for t in terms])


def put_sides(f_ref, acc, mine, theirs):
    acc = acc.astype(BF)
    count, rows, _ = mine.shape
    for side in range(2):

        @pl.when(f_ref[0] % 2 == side)
        def _():
            for z in range(count):
                at = 2 * z * rows
                mine[z] = acc[at + side * rows : at + (side + 1) * rows]
                theirs[z] = acc[at + (1 - side) * rows : at + (2 - side) * rows]


def mlp_gram_kernel(count, *refs):
    dys, n2s = refs[:count], refs[count : 2 * count]
    hid, gu = refs[2 * count : 3 * count], refs[3 * count : 4 * count]
    out = refs[-1]

    @pl.when(pl.program_id(0) == 0)
    def _():
        acc = dot_tn(dys[0][...], hid[0][...])
        for n in range(1, count):
            acc = acc + dot_tn(dys[n][...], hid[n][...])
        out[...] = acc.astype(out.dtype)

    @pl.when(pl.program_id(0) != 0)
    def _():
        acc = dot_tn(n2s[0][...], gu[0][0])
        for n in range(1, count):
            acc = acc + dot_tn(n2s[n][...], gu[n][0])
        out[...] = acc.astype(out.dtype)


def mlp_gram_call(dys, n2s, hid, gu, tile_m):
    rows, m = dys[0].shape
    k = hid[0].shape[1]
    count = len(dys)
    return pl.pallas_call(
        functools.partial(mlp_gram_kernel, count),
        grid=(3, m // tile_m),
        in_specs=[pl.BlockSpec((rows, tile_m), lambda j, i: (0, jnp.where(j == 0, i, m // tile_m - 1)))] * count
        + [pl.BlockSpec((rows, tile_m), lambda j, i: (0, jnp.where(j == 0, 0, i)))] * count
        + [pl.BlockSpec((rows, k), lambda j, i: (0, 0))] * count
        + [pl.BlockSpec((1, rows, k), lambda j, i: (jnp.maximum(j - 1, 0), 0, 0))] * count,
        out_specs=pl.BlockSpec((tile_m, k), lambda j, i: (i, j)),
        out_shape=jax.ShapeDtypeStruct((m, 3 * k), BF),
        compiler_params=params(56, ("arbitrary", "arbitrary")),
        cost_estimate=cost(18),
        name="mlp_gram",
    )(*dys, *n2s, *hid, *gu)


def gram_kernel(f_ref, left, right, mine, theirs):
    put_sides(f_ref, dot_tn(left[...], right[...]), mine, theirs)


def gram_call(f, left, right):
    rows, m = left.shape
    n = right.shape[1]
    one = pl.BlockSpec((2, m // 8, n), lambda i, f: (i, 0, 0))
    return pl.pallas_call(
        gram_kernel,
        grid_spec=pltpu.PrefetchScalarGridSpec(
            num_scalar_prefetch=1,
            grid=(2,),
            in_specs=[
                pl.BlockSpec((rows, m // 2), lambda i, f: (0, i)),
                pl.BlockSpec((rows, n), lambda i, f: (0, 0)),
            ],
            out_specs=[one, one],
        ),
        out_shape=[jax.ShapeDtypeStruct((4, m // 8, n), BF)] * 2,
        compiler_params=params(40, ("arbitrary",)),
        cost_estimate=cost(6),
        name="gram",
    )(f, left, right)


def out_gram_kernel(c_ref, f_ref, m0, m1, m2, m3, dattn, out):
    side = f_ref[0] % 2
    rows = out.shape[3]
    for d, ref in enumerate((m0, m1, m2, m3)):

        @pl.when(pl.program_id(0) == d)
        def _():
            tok = ref.shape[1] * ref.shape[2]
            acc = dot_tn(ref[0].reshape(tok, ref.shape[3]), dattn[...]).astype(BF)

            @pl.when(side == 0)
            def _():
                out[0, 0, 0] = acc[:rows]
                out[0, 1, 0] = acc[rows:]

            @pl.when(side != 0)
            def _():
                out[0, 0, 0] = acc[rows:]
                out[0, 1, 0] = acc[:rows]


def out_gram_call(c, f, mixed, r1, r2, dattn):
    seqs, tok, inner_w = mixed.shape[1:]
    rows, width = dattn.shape
    quarter = width // CTX

    def slot(n):
        return pl.BlockSpec((1, seqs, tok, inner_w), lambda d, e, c, f: (n, 0, 0, 0))

    return pl.pallas_call(
        out_gram_kernel,
        grid_spec=pltpu.PrefetchScalarGridSpec(
            num_scalar_prefetch=2,
            grid=(CTX, CTX),
            in_specs=[
                slot(0),
                slot(0),
                slot(0),
                slot(1),
                pl.BlockSpec((rows, quarter), lambda d, e, c, f: (0, e ^ c[0])),
            ],
            out_specs=pl.BlockSpec(
                (1, 2, 1, inner_w // 2, quarter), lambda d, e, c, f: (e, 0, d ^ c[0], 0, 0)
            ),
        ),
        out_shape=jax.ShapeDtypeStruct((CTX, 2, 4, inner_w // 2, quarter), BF),
        compiler_params=params(40, ("arbitrary", "arbitrary")),
        cost_estimate=cost(9),
        name="out_gram",
    )(c, f, mixed, r1, r2, r2, dattn)


def unpack_kernel(c_ref, s0, s1, s2, s3, perm, wq, wk, wv, gain, gq, gk, gv, gg, gm, go):
    c = c_ref[0]
    qw, kw = QH * HD, KH * HD
    n = perm.shape[0]
    g = gain[...]
    for b in range(CTX):
        for d, ref in enumerate((s0, s1, s2, s3)):

            @pl.when((b ^ c) == d)
            def _():
                flat = dot_nt(ref[:, :n], perm[...])
                gq[:, b * qw : (b + 1) * qw] = flat[:, :qw]
                gk[:, b * kw : (b + 1) * kw] = flat[:, qw : qw + kw]
                gv[:, b * kw : (b + 1) * kw] = flat[:, qw + kw :]
                go[:, b * qw : (b + 1) * qw] = ref[:, n : n + qw].astype(F32)

    total = jnp.zeros_like(g)
    for grad, w in ((gq, wq), (gk, wk), (gv, wv)):
        total = total + jnp.sum(grad[...] * w[...].astype(F32), axis=-1, keepdims=True)
        grad[...] = grad[...] * g
    gg[...] = total
    gm[...] = (
        s0[:, n + qw :].astype(F32)
        + s1[:, n + qw :].astype(F32)
        + s2[:, n + qw :].astype(F32)
        + s3[:, n + qw :].astype(F32)
    )[:, 0:1]


def unpack_call(c, parts, perm, wq, wk, wv, gain):
    rows = parts[0].shape[0]
    vm = pl.BlockSpec(memory_space=pltpu.VMEM)
    return pl.pallas_call(
        unpack_kernel,
        in_specs=[pl.BlockSpec(memory_space=pltpu.SMEM)] + [vm] * 9,
        out_specs=[vm] * 6,
        out_shape=[
            jax.ShapeDtypeStruct((rows, H * HD), F32),
            jax.ShapeDtypeStruct((rows, KVH * HD), F32),
            jax.ShapeDtypeStruct((rows, KVH * HD), F32),
            jax.ShapeDtypeStruct((rows, 1), F32),
            jax.ShapeDtypeStruct((rows, 1), F32),
            jax.ShapeDtypeStruct((rows, CTX * QH * HD), F32),
        ],
        compiler_params=pltpu.CompilerParams(vmem_limit_bytes=40 << 20),
        cost_estimate=cost(5),
        name="unpack",
    )(c, *parts, perm, wq, wk, wv, gain)


def qkv_back_kernel(c_ref, g, w, out):
    out[0, 0] = dot_nt(g[...], w[...]).astype(BF)


def qkv_back_call(c, grads, w, seqs, base):
    width = w.shape[0]
    return pl.pallas_call(
        qkv_back_kernel,
        grid_spec=pltpu.PrefetchScalarGridSpec(
            num_scalar_prefetch=1,
            grid=(2, seqs),
            in_specs=[
                pl.BlockSpec((BLK, 768), lambda d, s, c: (s * CTX + ((d + base) ^ c[0]), 0)),
                pl.BlockSpec((width, 768), lambda d, s, c: (0, 0)),
            ],
            out_specs=pl.BlockSpec((1, 1, BLK, width), lambda d, s, c: (d, s, 0, 0)),
        ),
        out_shape=jax.ShapeDtypeStruct((2, seqs, BLK, width), BF),
        compiler_params=params(40, ("arbitrary", "arbitrary")),
        cost_estimate=cost(3.3),
        name="qkv_back",
    )(c, grads, w)


def final_kernel(part_a, part_b, x, dresid, out):
    dn = part_a[0].astype(F32) + part_b[0].astype(F32)
    out[0] = dresid[0] + rms_back(x[0].astype(F32), dn)


def final_call(part_a, part_b, x, dresid):
    seqs, tok, width = x.shape
    tile = pl.BlockSpec((1, tok, width), lambda s: (s, 0, 0))
    return pl.pallas_call(
        final_kernel,
        grid=(seqs,),
        in_specs=[tile] * 4,
        out_specs=tile,
        out_shape=jax.ShapeDtypeStruct((seqs, tok, width), F32),
        compiler_params=params(40, ("arbitrary",)),
        cost_estimate=cost(4),
        name="final",
    )(part_a, part_b, x, dresid)


CORE = [(i, i ^ 1) for i in range(CTX)]
ROW = [(i, i ^ 2) for i in range(CTX)]


def swap_core(x):
    return lax.ppermute(x, "context", CORE)


def swap_row(x):
    return lax.ppermute(x, "context", ROW)


def gather_blocks(x):
    far = swap_row(x)
    near = swap_core(x)
    return [x, near, far, swap_core(far)]


def after(x, *first):
    return lax.optimization_barrier((x,) + first)[0]


def swap_fsdp(x, bit):
    size = lax.axis_size("fsdp")
    return lax.ppermute(x, "fsdp", [(i, i ^ bit) for i in range(size)])


def gather_fsdp(x):
    near = swap_fsdp(x, 2)
    side = swap_fsdp(x, 1)
    far = swap_fsdp(jnp.stack([x, near]), 4)
    near_side = swap_fsdp(near, 1)
    far_side = swap_fsdp(far, 1)
    return jnp.stack([x, side, near, near_side, far[0], far_side[0], far[1], far_side[1]])


def z_groups():
    size = lax.axis_size("fsdp")
    return [list(range(0, size, 2)), list(range(1, size, 2))]


def reduce_x(mine, theirs, *first):
    total = add_low(after(mine, *first), swap_fsdp(theirs, 1))
    return total.reshape(-1, total.shape[-1])


def reduce_z(x):
    return lax.psum_scatter(x, "fsdp", scatter_dimension=0, tiled=True, axis_index_groups=z_groups())


def add_low(a, b):
    return (a.astype(F32) + b.astype(F32)).astype(BF)


def on_device(
    tokens,
    segments,
    w_query,
    w_key,
    w_value,
    w_out,
    w_gate,
    w_up,
    w_down,
    gain_attn,
    gain_mlp,
    cotangent,
):
    seqs, tok, width = tokens.shape
    rows = seqs * tok
    length = tok * CTX
    qkv_w = (QH + 2 * KH) * HD
    ctx = lax.axis_index("context")
    core = ctx % 2
    c = ctx.astype(jnp.int32).reshape(1)

    last = []

    def step(call, x, *ready):
        x = after(x, *last, *ready)
        out = call(x)
        last[:] = [out[0] if isinstance(out, (tuple, list)) else out]
        return out

    segs = gather_blocks(segments)
    xs = gather_blocks(after(tokens, segs[2]))
    dys = gather_blocks(after(cotangent, xs[2]))

    perm = pack_matrix()
    fsdp = lax.axis_index("fsdp").astype(jnp.int32).reshape(1)
    col_a, col_m = gain_attn.astype(F32)[:, None], gain_mlp.astype(F32)[:, None]
    shard = jnp.concatenate(
        [
            lax.dynamic_slice_in_dim(w_query, ctx * (QH * HD), QH * HD, 1),
            lax.dynamic_slice_in_dim(w_key, ctx * (KH * HD), KH * HD, 1),
            lax.dynamic_slice_in_dim(w_value, ctx * (KH * HD), KH * HD, 1),
        ],
        axis=1,
    )
    shard = jnp.dot(shard, perm, preferred_element_type=F32)
    shard = (shard * col_a).astype(BF)
    quarter = width // CTX
    w_qkv = lax.all_gather(shard, "fsdp", axis=0, tiled=True)
    out_part = gather_fsdp(lax.dynamic_slice_in_dim(w_out, ctx * quarter, quarter, 1))
    out_parts = gather_blocks(out_part)
    down_t = jnp.transpose(w_down)
    ff = w_gate.shape[1] // 2
    w_parts = []
    for n in range(2):
        cols = slice(n * ff, (n + 1) * ff)
        part = jnp.concatenate(
            [
                (w_gate[:, cols].astype(F32) * col_m).astype(BF),
                (w_up[:, cols].astype(F32) * col_m).astype(BF),
                down_t[:, cols],
            ],
            axis=1,
        )
        part = after(part, *(segs[2:3] if n else [shard]))
        w_parts.append(lax.all_gather(part, "fsdp", axis=0, tiled=True))
    w_one, w_two = w_parts

    seg_blocks = jnp.stack(segs)
    whole_seg = jnp.concatenate(
        [lax.dynamic_index_in_dim(seg_blocks, b ^ ctx, 0, keepdims=False) for b in range(CTX)], axis=1
    )
    index = jnp.arange(length, dtype=jnp.int32)
    starts = jnp.concatenate(
        [jnp.ones((seqs, 1), dtype=bool), whole_seg[:, 1:] != whole_seg[:, :-1]], axis=1
    )
    first = lax.cummax(jnp.where(starts, index[None, :], 0), axis=1)
    positions = (index[None, :] - first).astype(F32).reshape(seqs * length, 1)
    freq = np.zeros((LANES,), np.float32)
    base = (THETA ** -(np.arange(HALF, dtype=np.float64) * 2.0 / HD)).astype(np.float32)
    for g in range(KH):
        freq[g * HALF : (g + 1) * HALF] = base
    angles = positions * jnp.asarray(freq)[None, :]
    cos, sin = jnp.cos(angles), jnp.sin(angles)
    low_block = (first[:, ::BLK] // BLK).reshape(seqs * CTX).astype(jnp.int32)
    first_rows = first.reshape(seqs, CTX, 1, BLK)

    normed, q, k, v = step(lambda t: qkv_call(c, xs, t, cos, sin), w_qkv, first_rows)
    mixed, lse = step(
        lambda t: attend_call(c, low_block, t, k, v, first_rows, seqs, length), q, dys[2]
    )
    r1 = swap_core(jnp.stack([mixed[1], mixed[3]]))
    r2 = swap_row(jnp.stack([mixed[2], r1[1]]))
    w_out_full = step(lambda t: assemble_call(c, fsdp, out_parts[:3] + [t]), out_parts[3])
    resid, normed_two = step(lambda t: out_call(c, tokens, mixed, r1, t, w_out_full), r2)

    n2s = [n.reshape(rows, width) for n in gather_blocks(normed_two)]
    dys = [d.reshape(rows, width) for d in dys]
    first_pairs = [step(lambda t: mlp_call(t, dys[d], w_one), n2s[d]) for d in range(CTX)]
    def gram(pairs, *ready):
        hid, gu = [p[0] for p in pairs], [p[1] for p in pairs]
        return step(lambda t: mlp_gram_call(dys, [t] + n2s[1:], hid, gu, 768), n2s[0], *ready)

    share_one = gram(first_pairs)
    s_one = lax.psum_scatter(share_one, "fsdp", scatter_dimension=0, tiled=True)
    second_pairs = [None] * CTX

    def back_rows(d, *ready):
        def call(t):
            terms = [(first_pairs[d][1], slot, w_one, slot) for slot in range(2)]
            return sum_nt_call(terms + [(t, slot, w_two, slot) for slot in range(2)], 512)

        return step(call, second_pairs[d][1], *ready)

    def down_rows(d, *ready):
        call = lambda t: sum_nt_call([(first_pairs[d][0], None, w_one, 2), (t, None, w_two, 2)], 512)
        return step(call, second_pairs[d][0], *ready)

    def back_pair(near, far, *ready):
        for d in (far, near):
            second_pairs[d] = step(lambda t: mlp_call(t, dys[d], w_two), n2s[d])
        low = back_rows(far)
        return back_rows(near, *ready), swap_core(low)

    dn2 = add_low(*back_pair(2, 3))
    dn_b = swap_row(dn2)
    last.append(dn2)
    dn_a = add_low(*back_pair(0, 1))
    share_two = gram(second_pairs)
    s_two = lax.psum_scatter(share_two, "fsdp", scatter_dimension=0, tiled=True)
    dresid, dattn, dmixed = step(
        lambda t: out_back_call(
            c, dn_a.reshape(tokens.shape), t.reshape(tokens.shape), resid, cotangent, w_out_full
        ),
        dn_b,
    )

    b1 = swap_core(jnp.stack([dmixed[1], dmixed[3]]))
    b2_send = jnp.stack([dmixed[2], b1[1]])
    b2 = swap_row(b2_send)
    g_out = step(lambda t: out_gram_call(c, fsdp, mixed, r1, r2, t), dattn.reshape(rows, width))
    got = swap_core(jnp.stack([g_out[1], g_out[3]]))
    g_send = add_low(g_out[2], got[1])
    low3, low2 = down_rows(3), down_rows(2)
    dqkv = step(
        lambda t: attend_back_call(
            c, low_block, q, k, v, mixed, dmixed, b1[0], t, lse, first_rows, cos, sin, seqs, length
        ),
        b2,
        g_send,
    )
    got_row = swap_row(after(g_send, b2))

    g_out = add_low(add_low(g_out[0], got[0]), after(got_row, dqkv))
    x_out = reduce_x(g_out[0], g_out[1])
    qkv_mine, qkv_theirs = step(lambda t: gram_call(fsdp, normed, t), dqkv, g_out)
    far = step(lambda t: qkv_back_call(c, t, w_qkv, seqs, 2), dqkv, x_out)
    dx2 = add_low(far[0], swap_core(far[1]))
    dx_b = swap_row(dx2)
    near = step(lambda t: qkv_back_call(c, t, w_qkv, seqs, 0), dqkv)
    dx_a = add_low(near[0], swap_core(near[1]))
    down2 = add_low(low2, swap_core(low3))
    down_b = swap_row(after(down2, got_row))
    low1, low0 = down_rows(1, down_b, dx2), down_rows(0)
    down_a = add_low(low0, swap_core(low1))
    x_all = jnp.concatenate([reduce_x(qkv_mine, qkv_theirs, near), x_out], axis=1)
    s_attn = reduce_z(x_all)
    grad_tokens = step(lambda t: final_call(dx_a, t, tokens, dresid), dx_b, x_all)
    s_down, s_gate, s_up = [
        jnp.concatenate([s[:, n * ff : (n + 1) * ff] for s in (s_one, s_two)], axis=1).astype(F32)
        for n in range(3)
    ]
    part_m = jnp.sum(s_gate * w_gate.astype(F32) + s_up * w_up.astype(F32), axis=1, keepdims=True)
    part_m = jnp.broadcast_to(part_m, (part_m.shape[0], LANES)).astype(BF)
    sums = gather_blocks(after(jnp.concatenate([s_attn, part_m], axis=1), grad_tokens))
    output = (
        resid + down_a.astype(F32).reshape(resid.shape) + down_b.astype(F32).reshape(resid.shape)
    ).astype(BF)
    g_query, g_key, g_value, g_gain_a, g_gain_m, g_w_out = step(
        lambda t: unpack_call(c, sums[:3] + [t], perm, w_query, w_key, w_value, col_a), sums[3]
    )
    return (
        output,
        grad_tokens,
        g_query,
        g_key,
        g_value,
        g_w_out,
        s_gate * col_m,
        s_up * col_m,
        jnp.transpose(s_down),
        g_gain_a[:, 0],
        g_gain_m[:, 0],
    )


def solution(mesh):
    split_heads = mesh.shape["context"] == CTX
    return jax.shard_map(
        on_device if split_heads else on_device_general,
        mesh=mesh,
        in_specs=(
            P("fsdp", "context", None),
            P("fsdp", "context"),
            P("fsdp", None),
            P("fsdp", None),
            P("fsdp", None),
            P("fsdp", None),
            P("fsdp", "context"),
            P("fsdp", "context"),
            P("context", "fsdp"),
            P("fsdp"),
            P("fsdp"),
            P("fsdp", "context", None),
        ),
        out_specs=(
            P("fsdp", "context", None),
            P("fsdp", "context", None),
            P("fsdp", None),
            P("fsdp", None),
            P("fsdp", None),
            P("fsdp", None),
            P("fsdp", "context"),
            P("fsdp", "context"),
            P("context", "fsdp"),
            P("fsdp"),
            P("fsdp"),
        ),
        check_vma=False,
    )
```

profile of v0, /device:TPU:1, one launch (start us, length us, event | category | flops | bytes accessed | tf_op | source)
XLA Modules:
  0.0 535.7 jit_solution(14364321647309273877)
XLA Ops:
  24.5 5.5 %multiply_sine_fusion = (f32[2048,128]{1,0:T(8,128)}, f32[2048,128]{1,0:T(8,128)}) fusion(f32[128]{0:T(128)S(1)} %copy-done.82, f32[2048]{0:T(1024)S(1)} %get-tuple-element.161), kind=kLoop, calls=%fused_computation.25 | loop fusion | flops 262144 | bytes 2105856 | tf_op jit(solution)/shard_map/sin | solution.py:1323
  32.8 25.8 %collective-permute-done.4.x2 = bf16[2,256,1536]{2,1,0:T(8,128)(2,1)} collective-permute-done((bf16[2,256,1536]{2,1,0:T(8,128)(2,1)}, bf16[2,256,1536]{2,1,0:T(8,128)(2,1)}, u32[]{:S(2)}, u32[]{:S(2)}) %collective-permute-start.4) | collective-permute-done | bytes 1572896 | tf_op jit(solution)/shard_map/ppermute | solution.py:1195
  62.7 7.7 %collective-permute-done.13 = bf16[2,192,384]{2,1,0:T(8,128)(2,1)S(1)} collective-permute-done((bf16[2,192,384]{2,1,0:T(8,128)(2,1)S(1)}, bf16[2,192,384]{2,1,0:T(8,128)(2,1)S(1)}, u32[]{:S(2)}, u32[]{:S(2)}) %collective-permute-start.13) | collective-permute-done | bytes 294944 | tf_op jit(solution)/shard_map/ppermute | solution.py:1210
  77.1 13.3 %qkv.1 = (bf16[2048,1536]{1,0:T(8,128)(2,1)}, bf16[2048,512]{1,0:T(8,128)(2,1)S(1)}, bf16[2048,256]{1,0:T(8,128)(2,1)S(1)}, bf16[2048,512]{1,0:T(8,128)(2,1)S(1)}) custom-call(s32[1]{0:T(128)} %bitcast.c_ref, bf16[2,256,1536]{2,1,0:T(8,128)(2,1)} %x.5, bf16[2,256,1536]{2,1,0:T(8,128)(2,1)} %collective-permute-done.3.x1, ...), custom_call_target="tpu_custom_call" | custom-call | flops 3737499904 | tf_op jit(solution)/shard_map/qkv/pallas_call | solution.py:492
  90.4 5.9 %collective-permute-done.6 = bf16[2,256,1536]{2,1,0:T(8,128)(2,1)} collective-permute-done((bf16[2,256,1536]{2,1,0:T(8,128)(2,1)S(1)}, bf16[2,256,1536]{2,1,0:T(8,128)(2,1)}, u32[]{:S(2)}, u32[]{:S(2)}) %collective-permute-start.6) | collective-permute-done | bytes 1572896 | tf_op jit(solution)/shard_map/ppermute | solution.py:1195
  96.3 18.0 %attend.1 = (bf16[4,2,256,384]{3,2,1,0:T(8,128)(2,1)S(1)}, f32[2,4,8,256]{3,2,1,0:T(8,128)S(1)}) custom-call(s32[8]{0:T(128)S(1)} %reshape.153.js_ref, s32[1]{0:T(128)} %bitcast.c_ref, bf16[2048,512]{1,0:T(8,128)(2,1)S(1)} %get-tuple-element.90.q, bf16[2048,256]{1,0:T(8,128)(2,1)S(1)} %get-tuple-element.91.k, bf16[2048,512]{1,0:T(8,128)(2,1)S(1)} %get-tuple-element.92.v, ...), custom_call_target="tpu_custom_call" | custom-call | flops 5175000064 | tf_op jit(solution)/shard_map/attend/pallas_call | solution.py:590
  116.7 4.9 collective-permute-done.15.p2
  126.9 5.5 %assemble.1.w = bf16[1536,1536]{1,0:T(8,128)(2,1)S(1)} custom-call(s32[1]{0:T(128)} %bitcast.c_ref, s32[1]{0:T(128)} %bitcast.11.f_ref, bf16[8,192,384]{2,1,0:T(8,128)(2,1)} %slice_dynamic-update-slice_fusion.p0, bf16[8,192,384]{2,1,0:T(8,128)(2,1)} %collective-permute-done.14.p1, bf16[8,192,384]{2,1,0:T(8,128)(2,1)} %collective-permute-done.15.p2, ...), custom_call_target="tpu_custom_call" | custom-call | flops 1437500032 | tf_op jit(solution)/shard_map/assemble/pallas_call | solution.py:777
  134.6 7.8 %collective-permute-done.8.m2.m3 = bf16[2,2,256,384]{3,2,1,0:T(8,128)(2,1)S(1)} collective-permute-done((bf16[2,2,256,384]{3,2,1,0:T(8,128)(2,1)}, bf16[2,2,256,384]{3,2,1,0:T(8,128)(2,1)S(1)}, u32[]{:S(2)}, u32[]{:S(2)}) %collective-permute-start.8) | collective-permute-done | bytes 786464 | tf_op jit(solution)/shard_map/ppermute | solution.py:1195
  142.4 7.8 %out_proj.1 = (f32[2,256,1536]{2,1,0:T(8,128)}, bf16[2,256,1536]{2,1,0:T(8,128)(2,1)}) custom-call(s32[1]{0:T(128)} %bitcast.c_ref, bf16[2,256,1536]{2,1,0:T(8,128)(2,1)} %x.5, bf16[4,2,256,384]{3,2,1,0:T(8,128)(2,1)} %copy-done.12, bf16[2,2,256,384]{3,2,1,0:T(8,128)(2,1)S(1)} %collective-permute-done.7.m1, ...), custom_call_target="tpu_custom_call" | custom-call | flops 2300000000 | tf_op jit(solution)/shard_map/out_proj/pallas_call | solution.py:810
  152.0 33.0 %collective-permute-done.18 = bf16[2,256,1536]{2,1,0:T(8,128)(2,1)} collective-permute-done((bf16[2,256,1536]{2,1,0:T(8,128)(2,1)}, bf16[2,256,1536]{2,1,0:T(8,128)(2,1)}, u32[]{:S(2)}, u32[]{:S(2)}) %collective-permute-start.18) | collective-permute-done | bytes 1572896 | tf_op jit(solution)/shard_map/ppermute | solution.py:1195
  189.6 4.7 mlp.8
  196.1 5.0 mlp.9
  203.0 5.0 mlp.10
  209.8 5.0 mlp.11
  216.6 18.0 %mlp_gram.2 = bf16[1536,1536]{1,0:T(8,128)(2,1)} custom-call(bf16[512,1536]{1,0:T(8,128)(2,1)} %bitcast.95, bf16[512,1536]{1,0:T(8,128)(2,1)} %bitcast.21.dy.refs_1_, bf16[512,1536]{1,0:T(8,128)(2,1)} %bitcast.22.dy.refs_2_, bf16[512,1536]{1,0:T(8,128)(2,1)} %bitcast.24.dy.refs_3_, bf16[512,1536]{1,0:T(8,128)(2,1)} %bitcast.16.n2.refs_4_, ...), custom_call_target="tpu_custom_call" | custom-call | flops 5175000064 | tf_op jit(solution)/shard_map/mlp_gram/pallas_call | solution.py:999
  238.2 5.2 mlp.12
  243.4 5.8 %mlp.13 = (bf16[512,512]{1,0:T(8,128)(2,1)S(1)}, bf16[2,512,512]{2,1,0:T(8,128)(2,1)S(1)}) custom-call(bf16[512,1536]{1,0:T(8,128)(2,1)} %bitcast.20.n2.refs_6_, bf16[512,1536]{1,0:T(8,128)(2,1)} %bitcast.22.dy.refs_2_, bf16[1536,1536]{1,0:T(8,128)(2,1)S(1)} %copy-done.4, bf16[1536,1536]{1,0:T(8,128)(2,1)S(1)} %copy-done.4, bf16[1536,1536]{1,0:T(8,128)(2,1)S(1)} %copy-done.4), custom_call_target="tpu_custom_call" | custom-call | flops 1293750016 | tf_op jit(solution)/shard_map/mlp/pallas_call | solution.py:904
  262.9 5.0 mlp.14
  268.8 5.0 mlp.15
  274.7 5.2 sum_nt.10
  285.8 17.7 %mlp_gram.3 = bf16[1536,1536]{1,0:T(8,128)(2,1)} custom-call(bf16[512,1536]{1,0:T(8,128)(2,1)} %bitcast.96, bf16[512,1536]{1,0:T(8,128)(2,1)} %bitcast.21.dy.refs_1_, bf16[512,1536]{1,0:T(8,128)(2,1)} %bitcast.22.dy.refs_2_, bf16[512,1536]{1,0:T(8,128)(2,1)} %bitcast.24.dy.refs_3_, bf16[512,1536]{1,0:T(8,128)(2,1)} %bitcast.16.n2.refs_4_, ...), custom_call_target="tpu_custom_call" | custom-call | flops 5175000064 | tf_op jit(solution)/shard_map/mlp_gram/pallas_call | solution.py:999
  307.9 9.6 %out_back.1 = (f32[2,256,1536]{2,1,0:T(8,128)}, bf16[2,256,1536]{2,1,0:T(8,128)(2,1)}, bf16[4,2,256,384]{3,2,1,0:T(8,128)(2,1)}) custom-call(s32[1]{0:T(128)} %bitcast.c_ref, bf16[2,256,1536]{2,1,0:T(8,128)(2,1)} %bitcast.103, bf16[2,256,1536]{2,1,0:T(8,128)(2,1)} %bitcast.26.part_b, f32[2,256,1536]{2,1,0:T(8,128)} %get-tuple-element.96.resid, ...), custom_call_target="tpu_custom_call" | custom-call | flops 2731249920 | tf_op jit(solution)/shard_map/out_back/pallas_call | solution.py:856
  318.9 8.6 %out_gram.1 = bf16[4,2,4,192,384]{4,3,2,1,0:T(8,128)(2,1)S(1)} custom-call(s32[1]{0:T(128)} %bitcast.c_ref, s32[1]{0:T(128)} %bitcast.11.f_ref, bf16[4,2,256,384]{3,2,1,0:T(8,128)(2,1)S(1)} %copy-done.13, bf16[2,2,256,384]{3,2,1,0:T(8,128)(2,1)S(1)} %copy-done.34, bf16[2,2,256,384]{3,2,1,0:T(8,128)(2,1)S(1)} %collective-permute-done.8.m2.m3, ...), custom_call_target="tpu_custom_call" | custom-call | flops 2587500032 | tf_op jit(solution)/shard_map/out_gram/pallas_call | solution.py:1069
  336.1 17.1 %collective-permute-done.26.d23 = bf16[2,2,256,384]{3,2,1,0:T(8,128)(2,1)S(1)} collective-permute-done((bf16[2,2,256,384]{3,2,1,0:T(8,128)(2,1)S(1)}, bf16[2,2,256,384]{3,2,1,0:T(8,128)(2,1)S(1)}, u32[]{:S(2)}, u32[]{:S(2)}) %collective-permute-start.26) | collective-permute-done | bytes 786464 | tf_op jit(solution)/shard_map/ppermute | solution.py:1195
  362.7 31.2 %attend_back.1.right.g = bf16[2048,768]{1,0:T(8,128)(2,1)} custom-call(s32[8]{0:T(128)S(1)} %reshape.153.js_ref, s32[1]{0:T(128)} %bitcast.c_ref, bf16[2048,512]{1,0:T(8,128)(2,1)} %copy-done.63, bf16[2048,256]{1,0:T(8,128)(2,1)S(1)} %copy-done.66, bf16[2048,512]{1,0:T(8,128)(2,1)} %copy-done.64, bf16[4,2,256,384]{3,2,1,0:T(8,128)(2,1)S(1)} %copy-done.13, ...), custom_call_target="tpu_custom_call" | custom-call | flops 8912499712 | tf_op jit(solution)/shard_map/attend_back/pallas_call | solution.py:729
  399.4 6.2 %gram.1 = (bf16[4,192,768]{2,1,0:T(8,128)(2,1)S(1)}, bf16[4,192,768]{2,1,0:T(8,128)(2,1)S(1)}) custom-call(s32[1]{0:T(128)} %bitcast.11.f_ref, bf16[2048,1536]{1,0:T(8,128)(2,1)S(1)} %copy-done.27, bf16[2048,768]{1,0:T(8,128)(2,1)S(1)} %copy-done.9), custom_call_target="tpu_custom_call" | custom-call | flops 1724999936 | tf_op jit(solution)/shard_map/gram/pallas_call | solution.py:1022
  407.0 5.5 %collective-permute-done.29 = bf16[4,192,384]{2,1,0:T(8,128)(2,1)S(1)} collective-permute-done((bf16[4,192,384]{2,1,0:T(8,128)(2,1)S(1)}, bf16[4,192,384]{2,1,0:T(8,128)(2,1)S(1)}, u32[]{:S(2)}, u32[]{:S(2)}) %collective-permute-start.29) | collective-permute-done | bytes 589856 | tf_op jit(solution)/shard_map/ppermute | solution.py:1210
  426.4 17.8 %collective-permute-done.36 = bf16[4,192,768]{2,1,0:T(8,128)(2,1)S(1)} collective-permute-done((bf16[4,192,768]{2,1,0:T(8,128)(2,1)S(1)}, bf16[4,192,768]{2,1,0:T(8,128)(2,1)S(1)}, u32[]{:S(2)}, u32[]{:S(2)}) %collective-permute-start.36) | collective-permute-done | bytes 1179680 | tf_op jit(solution)/shard_map/ppermute | solution.py:1210
  477.4 14.6 %collective-permute-done.35.part_b = bf16[2,256,1536]{2,1,0:T(8,128)(2,1)} collective-permute-done((bf16[2,256,1536]{2,1,0:T(8,128)(2,1)}, bf16[2,256,1536]{2,1,0:T(8,128)(2,1)}, u32[]{:S(2)}, u32[]{:S(2)}) %collective-permute-start.35) | collective-permute-done | bytes 1572896 | tf_op jit(solution)/shard_map/ppermute | solution.py:1195
  508.1 7.8 %collective-permute-done.38.s2 = bf16[192,1280]{1,0:T(8,128)(2,1)S(1)} collective-permute-done((bf16[192,1280]{1,0:T(8,128)(2,1)S(1)}, bf16[192,1280]{1,0:T(8,128)(2,1)S(1)}, u32[]{:S(2)}, u32[]{:S(2)}) %collective-permute-start.38) | collective-permute-done | bytes 491552 | tf_op jit(solution)/shard_map/ppermute | solution.py:1195
  522.0 5.1 unpack.1
  (348 shorter events, 179.7 us)
Async XLA Ops:
  7.2 67.4 %all-gather.4.cloned.1.call-start = ((), (), s32[]{:S(2)}) async-start(), calls=%async_computation.3 | async-start | bytes 2654208 | tf_op jit(solution)/shard_map/all_gather | solution.py:1288
  12.2 175.1 %all-gather.6.cloned.1.call-start = ((), (), s32[]{:S(2)}) async-start(), calls=%async_computation.4 | async-start | bytes 5308416 | tf_op jit(solution)/shard_map/all_gather | solution.py:1305
  13.7 222.2 %all-gather.8.cloned.1.call-start = ((), (), s32[]{:S(2)}) async-start(), calls=%async_computation.5 | async-start | bytes 5308416 | tf_op jit(solution)/shard_map/all_gather | solution.py:1305
  19.7 39.8 %collective-permute-start.9 = (bf16[192,384]{1,0:T(8,128)(2,1)S(1)}, bf16[192,384]{1,0:T(8,128)(2,1)S(1)}, u32[]{:S(2)}, u32[]{:S(2)}) collective-permute-start(bf16[192,384]{1,0:T(8,128)(2,1)S(1)} %get-tuple-element.160), channel_id=1, source_target_pairs={{0,4},{4,0},{8,12},{12,8},{16,20},{20,16},{24,28},{28,24},{1,5},{5... | collective-permute-start | bytes 442376 | tf_op jit(solution)/shard_map/ppermute | solution.py:1210
  22.4 36.3 %collective-permute-start.4 = (bf16[2,256,1536]{2,1,0:T(8,128)(2,1)}, bf16[2,256,1536]{2,1,0:T(8,128)(2,1)}, u32[]{:S(2)}, u32[]{:S(2)}) collective-permute-start(bf16[2,256,1536]{2,1,0:T(8,128)(2,1)} %x.5), channel_id=1, source_target_pairs={{0,2},{1,3},{2,0},{3,1},{4,6},{5,7},{6,4},{7,5},{8,10},{9,11},{10,... | collective-permute-start | bytes 4718600 | tf_op jit(solution)/shard_map/ppermute | solution.py:1195
  22.6 453.6 %reduce-scatter.6.cloned.1.call-start = ((), (), s32[]{:S(2)}) async-start(), calls=%async_computation.7 | async-start | bytes 5308416 | tf_op jit(solution)/shard_map/reduce_scatter | solution.py:1344
  22.7 51.9 %collective-permute-start.3 = (bf16[2,256,1536]{2,1,0:T(8,128)(2,1)}, bf16[2,256,1536]{2,1,0:T(8,128)(2,1)}, u32[]{:S(2)}, u32[]{:S(2)}) collective-permute-start(bf16[2,256,1536]{2,1,0:T(8,128)(2,1)} %x.5), channel_id=1, source_target_pairs={{0,1},{1,0},{2,3},{3,2},{4,5},{5,4},{6,7},{7,6},{8,9},{9,8},{10,11... | collective-permute-start | bytes 4718600 | tf_op jit(solution)/shard_map/ppermute | solution.py:1191
  30.2 30.9 %collective-permute-start.12 = (bf16[2,192,384]{2,1,0:T(8,128)(2,1)S(1)}, bf16[2,192,384]{2,1,0:T(8,128)(2,1)S(1)}, u32[]{:S(2)}, u32[]{:S(2)}) collective-permute-start(bf16[2,192,384]{2,1,0:T(8,128)(2,1)S(1)} %pad_maximum_fusion.11), channel_id=1, source_target_pairs={{0,16},{4,20},{8,24},{12,28},{16,0},{20,4},{24,8},{28,12},{1,17},{... | collective-permute-start | bytes 884744 | tf_op jit(solution)/shard_map/ppermute | solution.py:1210
  32.6 28.8 %collective-permute-start.11 = (bf16[192,384]{1,0:T(8,128)(2,1)S(1)}, bf16[192,384]{1,0:T(8,128)(2,1)S(1)}, u32[]{:S(2)}, u32[]{:S(2)}) collective-permute-start(bf16[192,384]{1,0:T(8,128)(2,1)S(1)} %collective-permute-done.10), channel_id=1, source_target_pairs={{0,4},{4,0},{8,12},{12,8},{16,20},{20,16},{24,28},{28,24},{1,5},{5... | collective-permute-start | bytes 442376 | tf_op jit(solution)/shard_map/ppermute | solution.py:1210
  58.6 16.0 %collective-permute-start.5 = (bf16[2,256,1536]{2,1,0:T(8,128)(2,1)}, bf16[2,256,1536]{2,1,0:T(8,128)(2,1)}, u32[]{:S(2)}, u32[]{:S(2)}) collective-permute-start(bf16[2,256,1536]{2,1,0:T(8,128)(2,1)} %collective-permute-done.4.x2), channel_id=1, source_target_pairs={{0,1},{1,0},{2,3},{3,2},{4,5},{5,4},{6,7},{7,6},{8,9},{9,8},{10,11... | collective-permute-start | bytes 4718600 | tf_op jit(solution)/shard_map/ppermute | solution.py:1191
  60.2 36.1 %collective-permute-start.6 = (bf16[2,256,1536]{2,1,0:T(8,128)(2,1)S(1)}, bf16[2,256,1536]{2,1,0:T(8,128)(2,1)}, u32[]{:S(2)}, u32[]{:S(2)}) collective-permute-start(bf16[2,256,1536]{2,1,0:T(8,128)(2,1)S(1)} %copy-done.7), channel_id=1, source_target_pairs={{0,2},{1,3},{2,0},{3,1},{4,6},{5,7},{6,4},{7,5},{8,10},{9,11},{10,... | collective-permute-start | bytes 4718600 | tf_op jit(solution)/shard_map/ppermute | solution.py:1195
  72.4 49.2 %collective-permute-start.15 = (bf16[8,192,384]{2,1,0:T(8,128)(2,1)}, bf16[8,192,384]{2,1,0:T(8,128)(2,1)}, u32[]{:S(2)}, u32[]{:S(2)}) collective-permute-start(bf16[8,192,384]{2,1,0:T(8,128)(2,1)} %slice_dynamic-update-slice_fusion.p0), channel_id=1, source_target_pairs={{0,2},{1,3},{2,0},{3,1},{4,6},{5,7},{6,4},{7,5},{8,10},{9,11},{10,... | collective-permute-start | bytes 3538952 | tf_op jit(solution)/shard_map/ppermute | solution.py:1195
  123.5 18.8 %collective-permute-start.8 = (bf16[2,2,256,384]{3,2,1,0:T(8,128)(2,1)}, bf16[2,2,256,384]{3,2,1,0:T(8,128)(2,1)S(1)}, u32[]{:S(2)}, u32[]{:S(2)}) collective-permute-start(bf16[2,2,256,384]{3,2,1,0:T(8,128)(2,1)} %pad_maximum_fusion.3), channel_id=1, source_target_pairs={{0,2},{1,3},{2,0},{3,1},{4,6},{5,7},{6,4},{7,5},{8,10},{9,11},{10,... | collective-permute-start | bytes 2359304 | tf_op jit(solution)/shard_map/ppermute | solution.py:1195
  150.2 34.9 %collective-permute-start.18 = (bf16[2,256,1536]{2,1,0:T(8,128)(2,1)}, bf16[2,256,1536]{2,1,0:T(8,128)(2,1)}, u32[]{:S(2)}, u32[]{:S(2)}) collective-permute-start(bf16[2,256,1536]{2,1,0:T(8,128)(2,1)} %get-tuple-element.97), channel_id=1, source_target_pairs={{0,2},{1,3},{2,0},{3,1},{4,6},{5,7},{6,4},{7,5},{8,10},{9,11},{10,... | collective-permute-start | bytes 4718600 | tf_op jit(solution)/shard_map/ppermute | solution.py:1195
  150.4 45.7 %collective-permute-start.17 = (bf16[2,256,1536]{2,1,0:T(8,128)(2,1)}, bf16[2,256,1536]{2,1,0:T(8,128)(2,1)}, u32[]{:S(2)}, u32[]{:S(2)}) collective-permute-start(bf16[2,256,1536]{2,1,0:T(8,128)(2,1)} %get-tuple-element.97), channel_id=1, source_target_pairs={{0,1},{1,0},{2,3},{3,2},{4,5},{5,4},{6,7},{7,6},{8,9},{9,8},{10,11... | collective-permute-start | bytes 4718600 | tf_op jit(solution)/shard_map/ppermute | solution.py:1191
  152.0 44.1 %collective-permute-start.19 = (bf16[2,256,1536]{2,1,0:T(8,128)(2,1)S(1)}, bf16[2,256,1536]{2,1,0:T(8,128)(2,1)}, u32[]{:S(2)}, u32[]{:S(2)}) collective-permute-start(bf16[2,256,1536]{2,1,0:T(8,128)(2,1)S(1)} %copy-done.7), channel_id=1, source_target_pairs={{0,1},{1,0},{2,3},{3,2},{4,5},{5,4},{6,7},{7,6},{8,9},{9,8},{10,11... | collective-permute-start | bytes 4718600 | tf_op jit(solution)/shard_map/ppermute | solution.py:1191
  185.0 24.7 %collective-permute-start.20 = (bf16[2,256,1536]{2,1,0:T(8,128)(2,1)}, bf16[2,256,1536]{2,1,0:T(8,128)(2,1)}, u32[]{:S(2)}, u32[]{:S(2)}) collective-permute-start(bf16[2,256,1536]{2,1,0:T(8,128)(2,1)} %collective-permute-done.18), channel_id=1, source_target_pairs={{0,1},{1,0},{2,3},{3,2},{4,5},{5,4},{6,7},{7,6},{8,9},{9,8},{10,11... | collective-permute-start | bytes 4718600 | tf_op jit(solution)/shard_map/ppermute | solution.py:1191
  187.3 22.5 %collective-permute-start.21 = (bf16[2,256,1536]{2,1,0:T(8,128)(2,1)}, bf16[2,256,1536]{2,1,0:T(8,128)(2,1)}, u32[]{:S(2)}, u32[]{:S(2)}) collective-permute-start(bf16[2,256,1536]{2,1,0:T(8,128)(2,1)} %collective-permute-done.6), channel_id=1, source_target_pairs={{0,1},{1,0},{2,3},{3,2},{4,5},{5,4},{6,7},{7,6},{8,9},{9,8},{10,11... | collective-permute-start | bytes 4718600 | tf_op jit(solution)/shard_map/ppermute | solution.py:1191
  234.6 264.6 %reduce-scatter.8.cloned.1.call-start = ((), (), s32[]{:S(2)}) async-start(), calls=%async_computation.8 | async-start | bytes 5308416 | tf_op jit(solution)/shard_map/reduce_scatter | solution.py:1369
  261.5 42.2 %collective-permute-start.24 = (bf16[512,1536]{1,0:T(8,128)(2,1)}, bf16[512,1536]{1,0:T(8,128)(2,1)}, u32[]{:S(2)}, u32[]{:S(2)}) collective-permute-start(bf16[512,1536]{1,0:T(8,128)(2,1)} %add_convert_fusion.3), channel_id=1, source_target_pairs={{0,2},{1,3},{2,0},{3,1},{4,6},{5,7},{6,4},{7,5},{8,10},{9,11},{10,... | collective-permute-start | bytes 4718600 | tf_op jit(solution)/shard_map/ppermute | solution.py:1195
  279.9 23.9 %collective-permute-start.23 = (bf16[512,1536]{1,0:T(8,128)(2,1)}, bf16[512,1536]{1,0:T(8,128)(2,1)}, u32[]{:S(2)}, u32[]{:S(2)}) collective-permute-start(bf16[512,1536]{1,0:T(8,128)(2,1)} %sum_nt.10), channel_id=1, source_target_pairs={{0,1},{1,0},{2,3},{3,2},{4,5},{5,4},{6,7},{7,6},{8,9},{9,8},{10,11... | collective-permute-start | bytes 4718600 | tf_op jit(solution)/shard_map/ppermute | solution.py:1191
  303.6 199.2 %reduce-scatter.4.cloned.1.call-start = ((), (), s32[]{:S(2)}) async-start(), calls=%async_computation.6 | async-start | bytes 2211840 | tf_op jit(solution)/shard_map/reduce_scatter | solution.py:1233
  334.2 18.9 %collective-permute-start.26 = (bf16[2,2,256,384]{3,2,1,0:T(8,128)(2,1)S(1)}, bf16[2,2,256,384]{3,2,1,0:T(8,128)(2,1)S(1)}, u32[]{:S(2)}, u32[]{:S(2)}) collective-permute-start(bf16[2,2,256,384]{3,2,1,0:T(8,128)(2,1)S(1)} %pad_maximum_fusion.5), channel_id=1, source_target_pairs={{0,2},{1,3},{2,0},{3,1},{4,6},{5,7},{6,4},{7,5},{8,10},{9,11},{10,... | collective-permute-start | bytes 2359304 | tf_op jit(solution)/shard_map/ppermute | solution.py:1195
  353.1 40.9 %collective-permute-start.28 = (bf16[2,4,192,384]{3,2,1,0:T(8,128)(2,1)}, bf16[2,4,192,384]{3,2,1,0:T(8,128)(2,1)}, u32[]{:S(2)}, u32[]{:S(2)}) collective-permute-start(bf16[2,4,192,384]{3,2,1,0:T(8,128)(2,1)} %fusion.8), channel_id=1, source_target_pairs={{0,2},{1,3},{2,0},{3,1},{4,6},{5,7},{6,4},{7,5},{8,10},{9,11},{10,... | collective-permute-start | bytes 3538952 | tf_op jit(solution)/shard_map/ppermute | solution.py:1195
  356.7 62.3 %collective-permute-start.30 = (bf16[512,1536]{1,0:T(8,128)(2,1)}, bf16[512,1536]{1,0:T(8,128)(2,1)}, u32[]{:S(2)}, u32[]{:S(2)}) collective-permute-start(bf16[512,1536]{1,0:T(8,128)(2,1)} %sum_nt.12), channel_id=1, source_target_pairs={{0,1},{1,0},{2,3},{3,2},{4,5},{5,4},{6,7},{7,6},{8,9},{9,8},{10,11... | collective-permute-start | bytes 4718600 | tf_op jit(solution)/shard_map/ppermute | solution.py:1191
  396.4 16.1 %collective-permute-start.29 = (bf16[4,192,384]{2,1,0:T(8,128)(2,1)S(1)}, bf16[4,192,384]{2,1,0:T(8,128)(2,1)S(1)}, u32[]{:S(2)}, u32[]{:S(2)}) collective-permute-start(bf16[4,192,384]{2,1,0:T(8,128)(2,1)S(1)} %get-tuple-element.172), channel_id=1, source_target_pairs={{0,4},{4,0},{8,12},{12,8},{16,20},{20,16},{24,28},{28,24},{1,5},{5... | collective-permute-start | bytes 1769480 | tf_op jit(solution)/shard_map/ppermute | solution.py:1210
  405.7 38.5 %collective-permute-start.36 = (bf16[4,192,768]{2,1,0:T(8,128)(2,1)S(1)}, bf16[4,192,768]{2,1,0:T(8,128)(2,1)S(1)}, u32[]{:S(2)}, u32[]{:S(2)}) collective-permute-start(bf16[4,192,768]{2,1,0:T(8,128)(2,1)S(1)} %get-tuple-element.149), channel_id=1, source_target_pairs={{0,4},{4,0},{8,12},{12,8},{16,20},{20,16},{24,28},{28,24},{1,5},{5... | collective-permute-start | bytes 3538952 | tf_op jit(solution)/shard_map/ppermute | solution.py:1210
  418.1 29.6 %collective-permute-start.32 = (bf16[2,256,1536]{2,1,0:T(8,128)(2,1)}, bf16[2,256,1536]{2,1,0:T(8,128)(2,1)}, u32[]{:S(2)}, u32[]{:S(2)}) collective-permute-start(bf16[2,256,1536]{2,1,0:T(8,128)(2,1)} %slice_bitcast_fusion.2), channel_id=1, source_target_pairs={{0,1},{1,0},{2,3},{3,2},{4,5},{5,4},{6,7},{7,6},{8,9},{9,8},{10,11... | collective-permute-start | bytes 4718600 | tf_op jit(solution)/shard_map/ppermute | solution.py:1191
  421.9 36.3 %collective-permute-start.31 = (bf16[512,1536]{1,0:T(8,128)(2,1)}, bf16[512,1536]{1,0:T(8,128)(2,1)}, u32[]{:S(2)}, u32[]{:S(2)}) collective-permute-start(bf16[512,1536]{1,0:T(8,128)(2,1)} %add_convert_fusion.1), channel_id=1, source_target_pairs={{0,2},{1,3},{2,0},{3,1},{4,6},{5,7},{6,4},{7,5},{8,10},{9,11},{10,... | collective-permute-start | bytes 4718600 | tf_op jit(solution)/shard_map/ppermute | solution.py:1195
  447.2 26.1 %collective-permute-start.34 = (bf16[2,256,1536]{2,1,0:T(8,128)(2,1)}, bf16[2,256,1536]{2,1,0:T(8,128)(2,1)}, u32[]{:S(2)}, u32[]{:S(2)}) collective-permute-start(bf16[2,256,1536]{2,1,0:T(8,128)(2,1)} %slice_bitcast_fusion), channel_id=1, source_target_pairs={{0,1},{1,0},{2,3},{3,2},{4,5},{5,4},{6,7},{7,6},{8,9},{9,8},{10,11... | collective-permute-start | bytes 4718600 | tf_op jit(solution)/shard_map/ppermute | solution.py:1191
  451.3 40.7 %collective-permute-start.35 = (bf16[2,256,1536]{2,1,0:T(8,128)(2,1)}, bf16[2,256,1536]{2,1,0:T(8,128)(2,1)}, u32[]{:S(2)}, u32[]{:S(2)}) collective-permute-start(bf16[2,256,1536]{2,1,0:T(8,128)(2,1)} %fusion.2), channel_id=1, source_target_pairs={{0,2},{1,3},{2,0},{3,1},{4,6},{5,7},{6,4},{7,5},{8,10},{9,11},{10,... | collective-permute-start | bytes 4718600 | tf_op jit(solution)/shard_map/ppermute | solution.py:1195
  468.3 36.8 %collective-permute-start.33 = (bf16[512,1536]{1,0:T(8,128)(2,1)}, bf16[512,1536]{1,0:T(8,128)(2,1)}, u32[]{:S(2)}, u32[]{:S(2)}) collective-permute-start(bf16[512,1536]{1,0:T(8,128)(2,1)} %sum_nt.14), channel_id=1, source_target_pairs={{0,1},{1,0},{2,3},{3,2},{4,5},{5,4},{6,7},{7,6},{8,9},{9,8},{10,11... | collective-permute-start | bytes 4718600 | tf_op jit(solution)/shard_map/ppermute | solution.py:1191
  (104 other events, 714.3 us)
Sparse Core Ops, SparseCore 0:
  12.3 62.2 all-gather.3
  77.4 77.0 all-gather.5
  157.3 78.5 all-gather.7
  239.3 94.3 reduce-scatter.5
  337.2 102.7 reduce-scatter.7
  446.0 37.9 reduce-scatter.3
where the time goes:
time: 547 us; the launch traced here: 536 us
  Pallas kernels  222 us (41%)
  waiting for transfers between devices  162 us (30%)
  local copies, waits for them, and re-layouts  56.6 us (10%)
  other arithmetic  41.3 us (8%)
  starting transfers between devices  35.9 us (7%)
  between operations  15.6 us (3%)
    ppermute x12, waiting for transfers between devices, swap_row(): return lax.ppermute(x, 'context', ROW)  121 us
    unnamed x190, local copies, waits for them, and re-layouts  46.8 us
    pallas_call x8, Pallas kernels, mlp_call(): pl.pallas_call(mlp_kernel, grid=(steps,), in_specs=[full, full, pl.BlockS...  40.7 us
    pallas_call x2, Pallas kernels, mlp_gram_call(): pl.pallas_call(functools.partial(mlp_gram_kernel, count), grid=(3, m // t...  35.7 us
    pallas_call x1, Pallas kernels, attend_back_call(): pl.pallas_call(attend_back_kernel, grid_spec=pltpu.PrefetchScalarGridSpec...  31.2 us
    ppermute x7, waiting for transfers between devices, swap_fsdp(): return lax.ppermute(x, 'fsdp', [(i, i ^ bit) for i in range(size)])  30.9 us
    pallas_call x8, Pallas kernels, sum_nt_call(): pl.pallas_call(functools.partial(sum_nt_kernel, tuple((t[1] for t in term...  30 us
    convert_element_type x10, other arithmetic, add_low(): return (a.astype(F32) + b.astype(F32)).astype(BF)  19.4 us
  transfers between devices with their start and end apart: 46, of which 18 were waited for; matrix products, arithmetic and copies ran while one was open for 10% of the time, Pallas kernels for 41%

commit v1 on v0

--- a/solution.py
+++ b/solution.py
@@ -1404,13 +1404,13 @@
     down_a = add_low(low0, swap_core(low1))
     x_all = jnp.concatenate([reduce_x(qkv_mine, qkv_theirs, near), x_out], axis=1)
     s_attn = reduce_z(x_all)
-    grad_tokens = step(lambda t: final_call(dx_a, t, tokens, dresid), dx_b, x_all)
     s_down, s_gate, s_up = [
         jnp.concatenate([s[:, n * ff : (n + 1) * ff] for s in (s_one, s_two)], axis=1).astype(F32)
         for n in range(3)
     ]
     part_m = jnp.sum(s_gate * w_gate.astype(F32) + s_up * w_up.astype(F32), axis=1, keepdims=True)
     part_m = jnp.broadcast_to(part_m, (part_m.shape[0], LANES)).astype(BF)
+    grad_tokens = step(lambda t: final_call(dx_a, t, tokens, dresid), dx_b, x_all, part_m)
     sums = gather_blocks(after(jnp.concatenate([s_attn, part_m], axis=1), grad_tokens))
     output = (
         resid + down_a.astype(F32).reshape(resid.shape) + down_b.astype(F32).reshape(resid.shape)

time: 547 us -> 538 us (0.984)
  local copies, waits for them, and re-layouts: 56.6 us -> 49.2 us
    unnamed x190 -> x180, local copies, waits for them, and re-layouts: 46.8 us -> 39.5 us
  transfers between devices with their start and end apart: 46 -> 46, of which waited for: 18 -> 16; matrix products, arithmetic and copies ran while one was open for 10% -> 10% of each run, Pallas kernels for 41% -> 41%
where the time goes in v1:
time: 538 us; the launch traced here: 527 us
  Pallas kernels  222 us (41%)
  waiting for transfers between devices  163 us (30%)
  local copies, waits for them, and re-layouts  49.2 us (9%)
  other arithmetic  41.7 us (8%)
  starting transfers between devices  33.5 us (6%)
  between operations  15.7 us (3%)
    ppermute x12, waiting for transfers between devices, swap_row(): return lax.ppermute(x, 'context', ROW)  120 us
    pallas_call x8, Pallas kernels, mlp_call(): pl.pallas_call(mlp_kernel, grid=(steps,), in_specs=[full, full, pl.BlockS...  41.2 us
    unnamed x180, local copies, waits for them, and re-layouts  39.5 us
    pallas_call x2, Pallas kernels, mlp_gram_call(): pl.pallas_call(functools.partial(mlp_gram_kernel, count), grid=(3, m // t...  36.1 us
    ppermute x7, waiting for transfers between devices, swap_fsdp(): return lax.ppermute(x, 'fsdp', [(i, i ^ bit) for i in range(size)])  34.1 us
    pallas_call x1, Pallas kernels, attend_back_call(): pl.pallas_call(attend_back_kernel, grid_spec=pltpu.PrefetchScalarGridSpec...  31.2 us
    pallas_call x8, Pallas kernels, sum_nt_call(): pl.pallas_call(functools.partial(sum_nt_kernel, tuple((t[1] for t in term...  29.2 us
    convert_element_type x10, other arithmetic, add_low(): return (a.astype(F32) + b.astype(F32)).astype(BF)  19.9 us
  transfers between devices with their start and end apart: 46, of which 16 were waited for; matrix products, arithmetic and copies ran while one was open for 10% of the time, Pallas kernels for 41%

profile of v1, /device:TPU:1, one launch (start us, length us, event | category | flops | bytes accessed | tf_op | source)
XLA Modules:
  0.0 527.0 jit_solution(4444000841612320051)
XLA Ops:
  24.5 5.5 %multiply_sine_fusion = (f32[2048,128]{1,0:T(8,128)}, f32[2048,128]{1,0:T(8,128)}) fusion(f32[128]{0:T(128)S(1)} %copy-done.77, f32[2048]{0:T(1024)S(1)} %get-tuple-element.161), kind=kLoop, calls=%fused_computation.25 | loop fusion | flops 262144 | bytes 2105856 | tf_op jit(solution)/shard_map/sin | solution.py:1323
  32.8 25.7 %collective-permute-done.4.x2 = bf16[2,256,1536]{2,1,0:T(8,128)(2,1)} collective-permute-done((bf16[2,256,1536]{2,1,0:T(8,128)(2,1)S(1)}, bf16[2,256,1536]{2,1,0:T(8,128)(2,1)}, u32[]{:S(2)}, u32[]{:S(2)}) %collective-permute-start.4) | collective-permute-done | bytes 1572896 | tf_op jit(solution)/shard_map/ppermute | solution.py:1195
  63.5 6.8 %collective-permute-done.13 = bf16[2,192,384]{2,1,0:T(8,128)(2,1)S(1)} collective-permute-done((bf16[2,192,384]{2,1,0:T(8,128)(2,1)S(1)}, bf16[2,192,384]{2,1,0:T(8,128)(2,1)S(1)}, u32[]{:S(2)}, u32[]{:S(2)}) %collective-permute-start.13) | collective-permute-done | bytes 294944 | tf_op jit(solution)/shard_map/ppermute | solution.py:1210
  76.0 13.0 %qkv.1 = (bf16[2048,1536]{1,0:T(8,128)(2,1)}, bf16[2048,512]{1,0:T(8,128)(2,1)S(1)}, bf16[2048,256]{1,0:T(8,128)(2,1)S(1)}, bf16[2048,512]{1,0:T(8,128)(2,1)S(1)}) custom-call(s32[1]{0:T(128)} %bitcast.c_ref, bf16[2,256,1536]{2,1,0:T(8,128)(2,1)S(1)} %copy-done.27, bf16[2,256,1536]{2,1,0:T(8,128)(2,1)} %collective-permute-done.3.x1, ...), custom_call_target="tpu_custom_call" | custom-call | flops 3737499904 | tf_op jit(solution)/shard_map/qkv/pallas_call | solution.py:492
  89.0 8.0 %collective-permute-done.6 = bf16[2,256,1536]{2,1,0:T(8,128)(2,1)} collective-permute-done((bf16[2,256,1536]{2,1,0:T(8,128)(2,1)S(1)}, bf16[2,256,1536]{2,1,0:T(8,128)(2,1)}, u32[]{:S(2)}, u32[]{:S(2)}) %collective-permute-start.6) | collective-permute-done | bytes 1572896 | tf_op jit(solution)/shard_map/ppermute | solution.py:1195
  97.1 18.0 %attend.1 = (bf16[4,2,256,384]{3,2,1,0:T(8,128)(2,1)S(1)}, f32[2,4,8,256]{3,2,1,0:T(8,128)S(1)}) custom-call(s32[8]{0:T(128)S(1)} %reshape.153.js_ref, s32[1]{0:T(128)} %bitcast.c_ref, bf16[2048,512]{1,0:T(8,128)(2,1)S(1)} %get-tuple-element.90.q, bf16[2048,256]{1,0:T(8,128)(2,1)S(1)} %get-tuple-element.91.k, bf16[2048,512]{1,0:T(8,128)(2,1)S(1)} %get-tuple-element.92.v, ...), custom_call_target="tpu_custom_call" | custom-call | flops 5175000064 | tf_op jit(solution)/shard_map/attend/pallas_call | solution.py:590
  117.4 5.0 collective-permute-done.15.p2
  127.6 5.6 %assemble.1.w = bf16[1536,1536]{1,0:T(8,128)(2,1)S(1)} custom-call(s32[1]{0:T(128)} %bitcast.c_ref, s32[1]{0:T(128)} %bitcast.11.f_ref, bf16[8,192,384]{2,1,0:T(8,128)(2,1)} %slice_dynamic-update-slice_fusion.p0, bf16[8,192,384]{2,1,0:T(8,128)(2,1)} %collective-permute-done.14.p1, bf16[8,192,384]{2,1,0:T(8,128)(2,1)} %collective-permute-done.15.p2, ...), custom_call_target="tpu_custom_call" | custom-call | flops 1437500032 | tf_op jit(solution)/shard_map/assemble/pallas_call | solution.py:777
  135.4 7.7 %collective-permute-done.8.m2.m3 = bf16[2,2,256,384]{3,2,1,0:T(8,128)(2,1)S(1)} collective-permute-done((bf16[2,2,256,384]{3,2,1,0:T(8,128)(2,1)}, bf16[2,2,256,384]{3,2,1,0:T(8,128)(2,1)S(1)}, u32[]{:S(2)}, u32[]{:S(2)}) %collective-permute-start.8) | collective-permute-done | bytes 786464 | tf_op jit(solution)/shard_map/ppermute | solution.py:1195
  143.1 7.6 %out_proj.1 = (f32[2,256,1536]{2,1,0:T(8,128)}, bf16[2,256,1536]{2,1,0:T(8,128)(2,1)}) custom-call(s32[1]{0:T(128)} %bitcast.c_ref, bf16[2,256,1536]{2,1,0:T(8,128)(2,1)S(1)} %copy-done.28, bf16[4,2,256,384]{3,2,1,0:T(8,128)(2,1)} %copy-done.11, bf16[2,2,256,384]{3,2,1,0:T(8,128)(2,1)S(1)} %collective-permute-done.7.m1, ...), custom_call_target="tpu_custom_call" | custom-call | flops 2300000000 | tf_op jit(solution)/shard_map/out_proj/pallas_call | solution.py:810
  152.4 33.2 %collective-permute-done.18 = bf16[2,256,1536]{2,1,0:T(8,128)(2,1)} collective-permute-done((bf16[2,256,1536]{2,1,0:T(8,128)(2,1)}, bf16[2,256,1536]{2,1,0:T(8,128)(2,1)}, u32[]{:S(2)}, u32[]{:S(2)}) %collective-permute-start.18) | collective-permute-done | bytes 1572896 | tf_op jit(solution)/shard_map/ppermute | solution.py:1195
  190.1 4.7 mlp.8
  194.9 5.3 %mlp.9 = (bf16[512,512]{1,0:T(8,128)(2,1)S(1)}, bf16[2,512,512]{2,1,0:T(8,128)(2,1)S(1)}) custom-call(bf16[512,1536]{1,0:T(8,128)(2,1)} %bitcast.19.n2.refs_5_, bf16[512,1536]{1,0:T(8,128)(2,1)} %bitcast.21.dy.refs_1_, bf16[1536,1536]{1,0:T(8,128)(2,1)S(1)} %copy-done.1, bf16[1536,1536]{1,0:T(8,128)(2,1)S(1)} %copy-done.1, bf16[1536,1536]{1,0:T(8,128)(2,1)S(1)} %copy-done.1), custom_call_target="tpu_custom_call" | custom-call | flops 1293750016 | tf_op jit(solution)/shard_map/mlp/pallas_call | solution.py:904
  202.0 5.0 mlp.10
  208.9 5.0 mlp.11
  215.7 18.2 %mlp_gram.2 = bf16[1536,1536]{1,0:T(8,128)(2,1)} custom-call(bf16[512,1536]{1,0:T(8,128)(2,1)} %bitcast.95, bf16[512,1536]{1,0:T(8,128)(2,1)} %bitcast.21.dy.refs_1_, bf16[512,1536]{1,0:T(8,128)(2,1)} %bitcast.22.dy.refs_2_, bf16[512,1536]{1,0:T(8,128)(2,1)} %bitcast.24.dy.refs_3_, bf16[512,1536]{1,0:T(8,128)(2,1)} %bitcast.16.n2.refs_4_, ...), custom_call_target="tpu_custom_call" | custom-call | flops 5175000064 | tf_op jit(solution)/shard_map/mlp_gram/pallas_call | solution.py:999
  237.5 5.2 mlp.12
  243.5 5.9 %mlp.13 = (bf16[512,512]{1,0:T(8,128)(2,1)S(1)}, bf16[2,512,512]{2,1,0:T(8,128)(2,1)S(1)}) custom-call(bf16[512,1536]{1,0:T(8,128)(2,1)} %bitcast.20.n2.refs_6_, bf16[512,1536]{1,0:T(8,128)(2,1)} %bitcast.22.dy.refs_2_, bf16[1536,1536]{1,0:T(8,128)(2,1)S(1)} %copy-done.4, bf16[1536,1536]{1,0:T(8,128)(2,1)S(1)} %copy-done.4, bf16[1536,1536]{1,0:T(8,128)(2,1)S(1)} %copy-done.4), custom_call_target="tpu_custom_call" | custom-call | flops 1293750016 | tf_op jit(solution)/shard_map/mlp/pallas_call | solution.py:904
  262.6 5.1 mlp.14
  268.5 5.0 mlp.15
  273.5 5.2 sum_nt.10
  283.5 18.0 %mlp_gram.3 = bf16[1536,1536]{1,0:T(8,128)(2,1)} custom-call(bf16[512,1536]{1,0:T(8,128)(2,1)} %bitcast.96, bf16[512,1536]{1,0:T(8,128)(2,1)} %bitcast.21.dy.refs_1_, bf16[512,1536]{1,0:T(8,128)(2,1)} %bitcast.22.dy.refs_2_, bf16[512,1536]{1,0:T(8,128)(2,1)} %bitcast.24.dy.refs_3_, bf16[512,1536]{1,0:T(8,128)(2,1)} %bitcast.16.n2.refs_4_, ...), custom_call_target="tpu_custom_call" | custom-call | flops 5175000064 | tf_op jit(solution)/shard_map/mlp_gram/pallas_call | solution.py:999
  304.7 9.5 %out_back.1 = (f32[2,256,1536]{2,1,0:T(8,128)}, bf16[2,256,1536]{2,1,0:T(8,128)(2,1)}, bf16[4,2,256,384]{3,2,1,0:T(8,128)(2,1)}) custom-call(s32[1]{0:T(128)} %bitcast.c_ref, bf16[2,256,1536]{2,1,0:T(8,128)(2,1)} %bitcast.103, bf16[2,256,1536]{2,1,0:T(8,128)(2,1)} %bitcast.26.part_b, f32[2,256,1536]{2,1,0:T(8,128)} %get-tuple-element.96.resid, ...), custom_call_target="tpu_custom_call" | custom-call | flops 2731249920 | tf_op jit(solution)/shard_map/out_back/pallas_call | solution.py:856
  315.6 8.6 %out_gram.1 = bf16[4,2,4,192,384]{4,3,2,1,0:T(8,128)(2,1)S(1)} custom-call(s32[1]{0:T(128)} %bitcast.c_ref, s32[1]{0:T(128)} %bitcast.11.f_ref, bf16[4,2,256,384]{3,2,1,0:T(8,128)(2,1)S(1)} %copy-done.12, bf16[2,2,256,384]{3,2,1,0:T(8,128)(2,1)S(1)} %collective-permute-done.7.m1, bf16[2,2,256,384]{3,2,1,0:T(8,128)(2,1)S(1)} %collective-permute-done.8.m2.m3, ...), custom_call_target="tpu_custom_call" | custom-call | flops 2587500032 | tf_op jit(solution)/shard_map/out_gram/pallas_call | solution.py:1069
  332.9 17.1 %collective-permute-done.26.d23 = bf16[2,2,256,384]{3,2,1,0:T(8,128)(2,1)S(1)} collective-permute-done((bf16[2,2,256,384]{3,2,1,0:T(8,128)(2,1)S(1)}, bf16[2,2,256,384]{3,2,1,0:T(8,128)(2,1)S(1)}, u32[]{:S(2)}, u32[]{:S(2)}) %collective-permute-start.26) | collective-permute-done | bytes 786464 | tf_op jit(solution)/shard_map/ppermute | solution.py:1195
  359.1 31.2 %attend_back.1.right.g = bf16[2048,768]{1,0:T(8,128)(2,1)} custom-call(s32[8]{0:T(128)S(1)} %reshape.153.js_ref, s32[1]{0:T(128)} %bitcast.c_ref, bf16[2048,512]{1,0:T(8,128)(2,1)} %copy-done.59, bf16[2048,256]{1,0:T(8,128)(2,1)S(1)} %copy-done.62, bf16[2048,512]{1,0:T(8,128)(2,1)} %copy-done.60, bf16[4,2,256,384]{3,2,1,0:T(8,128)(2,1)S(1)} %copy-done.12, ...), custom_call_target="tpu_custom_call" | custom-call | flops 8912499712 | tf_op jit(solution)/shard_map/attend_back/pallas_call | solution.py:729
  395.8 6.2 %gram.1 = (bf16[4,192,768]{2,1,0:T(8,128)(2,1)S(1)}, bf16[4,192,768]{2,1,0:T(8,128)(2,1)S(1)}) custom-call(s32[1]{0:T(128)} %bitcast.11.f_ref, bf16[2048,1536]{1,0:T(8,128)(2,1)S(1)} %copy-done.26, bf16[2048,768]{1,0:T(8,128)(2,1)S(1)} %copy-done.9), custom_call_target="tpu_custom_call" | custom-call | flops 1724999936 | tf_op jit(solution)/shard_map/gram/pallas_call | solution.py:1022
  407.3 4.6 collective-permute-done.29
  420.6 22.7 %collective-permute-done.36 = bf16[4,192,768]{2,1,0:T(8,128)(2,1)S(1)} collective-permute-done((bf16[4,192,768]{2,1,0:T(8,128)(2,1)S(1)}, bf16[4,192,768]{2,1,0:T(8,128)(2,1)S(1)}, u32[]{:S(2)}, u32[]{:S(2)}) %collective-permute-start.36) | collective-permute-done | bytes 1179680 | tf_op jit(solution)/shard_map/ppermute | solution.py:1210
  473.0 15.5 %collective-permute-done.35.part_b = bf16[2,256,1536]{2,1,0:T(8,128)(2,1)} collective-permute-done((bf16[2,256,1536]{2,1,0:T(8,128)(2,1)}, bf16[2,256,1536]{2,1,0:T(8,128)(2,1)}, u32[]{:S(2)}, u32[]{:S(2)}) %collective-permute-start.35) | collective-permute-done | bytes 1572896 | tf_op jit(solution)/shard_map/ppermute | solution.py:1195
  499.4 7.8 %collective-permute-done.38.s2 = bf16[192,1280]{1,0:T(8,128)(2,1)S(1)} collective-permute-done((bf16[192,1280]{1,0:T(8,128)(2,1)S(1)}, bf16[192,1280]{1,0:T(8,128)(2,1)S(1)}, u32[]{:S(2)}, u32[]{:S(2)}) %collective-permute-start.38) | collective-permute-done | bytes 491552 | tf_op jit(solution)/shard_map/ppermute | solution.py:1195
  513.3 5.1 unpack.1
  (338 shorter events, 164.5 us)
Async XLA Ops:
  7.2 66.4 %all-gather.4.cloned.1.call-start = ((), (), s32[]{:S(2)}) async-start(), calls=%async_computation.3 | async-start | bytes 2654208 | tf_op jit(solution)/shard_map/all_gather | solution.py:1288
  12.2 175.6 %all-gather.6.cloned.1.call-start = ((), (), s32[]{:S(2)}) async-start(), calls=%async_computation.4 | async-start | bytes 5308416 | tf_op jit(solution)/shard_map/all_gather | solution.py:1305
  13.7 221.5 %all-gather.8.cloned.1.call-start = ((), (), s32[]{:S(2)}) async-start(), calls=%async_computation.5 | async-start | bytes 5308416 | tf_op jit(solution)/shard_map/all_gather | solution.py:1305
  19.7 39.6 %collective-permute-start.9 = (bf16[192,384]{1,0:T(8,128)(2,1)S(1)}, bf16[192,384]{1,0:T(8,128)(2,1)}, u32[]{:S(2)}, u32[]{:S(2)}) collective-permute-start(bf16[192,384]{1,0:T(8,128)(2,1)S(1)} %get-tuple-element.160), channel_id=1, source_target_pairs={{0,4},{4,0},{8,12},{12,8},{16,20},{20,16},{24,28},{28,24},{1,5},{5... | collective-permute-start | bytes 442376 | tf_op jit(solution)/shard_map/ppermute | solution.py:1210
  22.4 36.2 %collective-permute-start.4 = (bf16[2,256,1536]{2,1,0:T(8,128)(2,1)S(1)}, bf16[2,256,1536]{2,1,0:T(8,128)(2,1)}, u32[]{:S(2)}, u32[]{:S(2)}) collective-permute-start(bf16[2,256,1536]{2,1,0:T(8,128)(2,1)S(1)} %copy-done.27), channel_id=1, source_target_pairs={{0,2},{1,3},{2,0},{3,1},{4,6},{5,7},{6,4},{7,5},{8,10},{9,11},{10,... | collective-permute-start | bytes 4718600 | tf_op jit(solution)/shard_map/ppermute | solution.py:1195
  22.7 445.5 %reduce-scatter.4.cloned.1.call-start = ((), (), s32[]{:S(2)}) async-start(), calls=%async_computation.6 | async-start | bytes 5308416 | tf_op jit(solution)/shard_map/reduce_scatter | solution.py:1344
  22.7 50.8 %collective-permute-start.3 = (bf16[2,256,1536]{2,1,0:T(8,128)(2,1)S(1)}, bf16[2,256,1536]{2,1,0:T(8,128)(2,1)}, u32[]{:S(2)}, u32[]{:S(2)}) collective-permute-start(bf16[2,256,1536]{2,1,0:T(8,128)(2,1)S(1)} %copy-done.27), channel_id=1, source_target_pairs={{0,1},{1,0},{2,3},{3,2},{4,5},{5,4},{6,7},{7,6},{8,9},{9,8},{10,11... | collective-permute-start | bytes 4718600 | tf_op jit(solution)/shard_map/ppermute | solution.py:1191
  30.2 31.6 %collective-permute-start.12 = (bf16[2,192,384]{2,1,0:T(8,128)(2,1)S(1)}, bf16[2,192,384]{2,1,0:T(8,128)(2,1)S(1)}, u32[]{:S(2)}, u32[]{:S(2)}) collective-permute-start(bf16[2,192,384]{2,1,0:T(8,128)(2,1)S(1)} %pad_maximum_fusion.11), channel_id=1, source_target_pairs={{0,16},{4,20},{8,24},{12,28},{16,0},{20,4},{24,8},{28,12},{1,17},{... | collective-permute-start | bytes 884744 | tf_op jit(solution)/shard_map/ppermute | solution.py:1210
  32.6 29.5 %collective-permute-start.11 = (bf16[192,384]{1,0:T(8,128)(2,1)S(1)}, bf16[192,384]{1,0:T(8,128)(2,1)S(1)}, u32[]{:S(2)}, u32[]{:S(2)}) collective-permute-start(bf16[192,384]{1,0:T(8,128)(2,1)S(1)} %collective-permute-done.10), channel_id=1, source_target_pairs={{0,4},{4,0},{8,12},{12,8},{16,20},{20,16},{24,28},{28,24},{1,5},{5... | collective-permute-start | bytes 442376 | tf_op jit(solution)/shard_map/ppermute | solution.py:1210
  58.5 15.0 %collective-permute-start.5 = (bf16[2,256,1536]{2,1,0:T(8,128)(2,1)}, bf16[2,256,1536]{2,1,0:T(8,128)(2,1)}, u32[]{:S(2)}, u32[]{:S(2)}) collective-permute-start(bf16[2,256,1536]{2,1,0:T(8,128)(2,1)} %collective-permute-done.4.x2), channel_id=1, source_target_pairs={{0,1},{1,0},{2,3},{3,2},{4,5},{5,4},{6,7},{7,6},{8,9},{9,8},{10,11... | collective-permute-start | bytes 4718600 | tf_op jit(solution)/shard_map/ppermute | solution.py:1191
  60.9 36.1 %collective-permute-start.6 = (bf16[2,256,1536]{2,1,0:T(8,128)(2,1)S(1)}, bf16[2,256,1536]{2,1,0:T(8,128)(2,1)}, u32[]{:S(2)}, u32[]{:S(2)}) collective-permute-start(bf16[2,256,1536]{2,1,0:T(8,128)(2,1)S(1)} %copy-done.7), channel_id=1, source_target_pairs={{0,2},{1,3},{2,0},{3,1},{4,6},{5,7},{6,4},{7,5},{8,10},{9,11},{10,... | collective-permute-start | bytes 4718600 | tf_op jit(solution)/shard_map/ppermute | solution.py:1195
  72.3 50.0 %collective-permute-start.15 = (bf16[8,192,384]{2,1,0:T(8,128)(2,1)}, bf16[8,192,384]{2,1,0:T(8,128)(2,1)}, u32[]{:S(2)}, u32[]{:S(2)}) collective-permute-start(bf16[8,192,384]{2,1,0:T(8,128)(2,1)} %slice_dynamic-update-slice_fusion.p0), channel_id=1, source_target_pairs={{0,2},{1,3},{2,0},{3,1},{4,6},{5,7},{6,4},{7,5},{8,10},{9,11},{10,... | collective-permute-start | bytes 3538952 | tf_op jit(solution)/shard_map/ppermute | solution.py:1195
  124.1 18.9 %collective-permute-start.8 = (bf16[2,2,256,384]{3,2,1,0:T(8,128)(2,1)}, bf16[2,2,256,384]{3,2,1,0:T(8,128)(2,1)S(1)}, u32[]{:S(2)}, u32[]{:S(2)}) collective-permute-start(bf16[2,2,256,384]{3,2,1,0:T(8,128)(2,1)} %pad_maximum_fusion.3), channel_id=1, source_target_pairs={{0,2},{1,3},{2,0},{3,1},{4,6},{5,7},{6,4},{7,5},{8,10},{9,11},{10,... | collective-permute-start | bytes 2359304 | tf_op jit(solution)/shard_map/ppermute | solution.py:1195
  150.6 34.9 %collective-permute-start.18 = (bf16[2,256,1536]{2,1,0:T(8,128)(2,1)}, bf16[2,256,1536]{2,1,0:T(8,128)(2,1)}, u32[]{:S(2)}, u32[]{:S(2)}) collective-permute-start(bf16[2,256,1536]{2,1,0:T(8,128)(2,1)} %get-tuple-element.97), channel_id=1, source_target_pairs={{0,2},{1,3},{2,0},{3,1},{4,6},{5,7},{6,4},{7,5},{8,10},{9,11},{10,... | collective-permute-start | bytes 4718600 | tf_op jit(solution)/shard_map/ppermute | solution.py:1195
  150.8 44.1 %collective-permute-start.17 = (bf16[2,256,1536]{2,1,0:T(8,128)(2,1)}, bf16[2,256,1536]{2,1,0:T(8,128)(2,1)}, u32[]{:S(2)}, u32[]{:S(2)}) collective-permute-start(bf16[2,256,1536]{2,1,0:T(8,128)(2,1)} %get-tuple-element.97), channel_id=1, source_target_pairs={{0,1},{1,0},{2,3},{3,2},{4,5},{5,4},{6,7},{7,6},{8,9},{9,8},{10,11... | collective-permute-start | bytes 4718600 | tf_op jit(solution)/shard_map/ppermute | solution.py:1191
  152.4 42.4 %collective-permute-start.19 = (bf16[2,256,1536]{2,1,0:T(8,128)(2,1)S(1)}, bf16[2,256,1536]{2,1,0:T(8,128)(2,1)}, u32[]{:S(2)}, u32[]{:S(2)}) collective-permute-start(bf16[2,256,1536]{2,1,0:T(8,128)(2,1)S(1)} %copy-done.7), channel_id=1, source_target_pairs={{0,1},{1,0},{2,3},{3,2},{4,5},{5,4},{6,7},{7,6},{8,9},{9,8},{10,11... | collective-permute-start | bytes 4718600 | tf_op jit(solution)/shard_map/ppermute | solution.py:1191
  185.6 23.3 %collective-permute-start.20 = (bf16[2,256,1536]{2,1,0:T(8,128)(2,1)}, bf16[2,256,1536]{2,1,0:T(8,128)(2,1)}, u32[]{:S(2)}, u32[]{:S(2)}) collective-permute-start(bf16[2,256,1536]{2,1,0:T(8,128)(2,1)} %collective-permute-done.18), channel_id=1, source_target_pairs={{0,1},{1,0},{2,3},{3,2},{4,5},{5,4},{6,7},{7,6},{8,9},{9,8},{10,11... | collective-permute-start | bytes 4718600 | tf_op jit(solution)/shard_map/ppermute | solution.py:1191
  187.8 21.1 %collective-permute-start.21 = (bf16[2,256,1536]{2,1,0:T(8,128)(2,1)}, bf16[2,256,1536]{2,1,0:T(8,128)(2,1)}, u32[]{:S(2)}, u32[]{:S(2)}) collective-permute-start(bf16[2,256,1536]{2,1,0:T(8,128)(2,1)} %collective-permute-done.6), channel_id=1, source_target_pairs={{0,1},{1,0},{2,3},{3,2},{4,5},{5,4},{6,7},{7,6},{8,9},{9,8},{10,11... | collective-permute-start | bytes 4718600 | tf_op jit(solution)/shard_map/ppermute | solution.py:1191
  233.8 235.6 %reduce-scatter.6.cloned.1.call-start = ((), (), s32[]{:S(2)}) async-start(), calls=%async_computation.7 | async-start | bytes 5308416 | tf_op jit(solution)/shard_map/reduce_scatter | solution.py:1369
  261.3 40.4 %collective-permute-start.24 = (bf16[512,1536]{1,0:T(8,128)(2,1)}, bf16[512,1536]{1,0:T(8,128)(2,1)}, u32[]{:S(2)}, u32[]{:S(2)}) collective-permute-start(bf16[512,1536]{1,0:T(8,128)(2,1)} %add_convert_fusion.3), channel_id=1, source_target_pairs={{0,2},{1,3},{2,0},{3,1},{4,6},{5,7},{6,4},{7,5},{8,10},{9,11},{10,... | collective-permute-start | bytes 4718600 | tf_op jit(solution)/shard_map/ppermute | solution.py:1195
  278.7 23.0 %collective-permute-start.23 = (bf16[512,1536]{1,0:T(8,128)(2,1)}, bf16[512,1536]{1,0:T(8,128)(2,1)}, u32[]{:S(2)}, u32[]{:S(2)}) collective-permute-start(bf16[512,1536]{1,0:T(8,128)(2,1)} %sum_nt.10), channel_id=1, source_target_pairs={{0,1},{1,0},{2,3},{3,2},{4,5},{5,4},{6,7},{7,6},{8,9},{9,8},{10,11... | collective-permute-start | bytes 4718600 | tf_op jit(solution)/shard_map/ppermute | solution.py:1191
  301.5 192.7 %reduce-scatter.8.cloned.1.call-start = ((), (), s32[]{:S(2)}) async-start(), calls=%async_computation.8 | async-start | bytes 2211840 | tf_op jit(solution)/shard_map/reduce_scatter | solution.py:1233
  330.8 19.1 %collective-permute-start.26 = (bf16[2,2,256,384]{3,2,1,0:T(8,128)(2,1)S(1)}, bf16[2,2,256,384]{3,2,1,0:T(8,128)(2,1)S(1)}, u32[]{:S(2)}, u32[]{:S(2)}) collective-permute-start(bf16[2,2,256,384]{3,2,1,0:T(8,128)(2,1)S(1)} %pad_maximum_fusion.5), channel_id=1, source_target_pairs={{0,2},{1,3},{2,0},{3,1},{4,6},{5,7},{6,4},{7,5},{8,10},{9,11},{10,... | collective-permute-start | bytes 2359304 | tf_op jit(solution)/shard_map/ppermute | solution.py:1195
  349.9 40.3 %collective-permute-start.28 = (bf16[2,4,192,384]{3,2,1,0:T(8,128)(2,1)}, bf16[2,4,192,384]{3,2,1,0:T(8,128)(2,1)}, u32[]{:S(2)}, u32[]{:S(2)}) collective-permute-start(bf16[2,4,192,384]{3,2,1,0:T(8,128)(2,1)} %fusion.8), channel_id=1, source_target_pairs={{0,2},{1,3},{2,0},{3,1},{4,6},{5,7},{6,4},{7,5},{8,10},{9,11},{10,... | collective-permute-start | bytes 3538952 | tf_op jit(solution)/shard_map/ppermute | solution.py:1195
  352.8 50.2 %collective-permute-start.30 = (bf16[512,1536]{1,0:T(8,128)(2,1)S(1)}, bf16[512,1536]{1,0:T(8,128)(2,1)}, u32[]{:S(2)}, u32[]{:S(2)}) collective-permute-start(bf16[512,1536]{1,0:T(8,128)(2,1)S(1)} %sum_nt.12), channel_id=1, source_target_pairs={{0,1},{1,0},{2,3},{3,2},{4,5},{5,4},{6,7},{7,6},{8,9},{9,8},{10,11... | collective-permute-start | bytes 4718600 | tf_op jit(solution)/shard_map/ppermute | solution.py:1191
  392.3 19.5 %collective-permute-start.29 = (bf16[4,192,384]{2,1,0:T(8,128)(2,1)S(1)}, bf16[4,192,384]{2,1,0:T(8,128)(2,1)S(1)}, u32[]{:S(2)}, u32[]{:S(2)}) collective-permute-start(bf16[4,192,384]{2,1,0:T(8,128)(2,1)S(1)} %get-tuple-element.172), channel_id=1, source_target_pairs={{0,4},{4,0},{8,12},{12,8},{16,20},{20,16},{24,28},{28,24},{1,5},{5... | collective-permute-start | bytes 1769480 | tf_op jit(solution)/shard_map/ppermute | solution.py:1210
  402.0 41.3 %collective-permute-start.36 = (bf16[4,192,768]{2,1,0:T(8,128)(2,1)S(1)}, bf16[4,192,768]{2,1,0:T(8,128)(2,1)S(1)}, u32[]{:S(2)}, u32[]{:S(2)}) collective-permute-start(bf16[4,192,768]{2,1,0:T(8,128)(2,1)S(1)} %get-tuple-element.149), channel_id=1, source_target_pairs={{0,4},{4,0},{8,12},{12,8},{16,20},{20,16},{24,28},{28,24},{1,5},{5... | collective-permute-start | bytes 3538952 | tf_op jit(solution)/shard_map/ppermute | solution.py:1210
  406.1 47.2 %collective-permute-start.31 = (bf16[512,1536]{1,0:T(8,128)(2,1)}, bf16[512,1536]{1,0:T(8,128)(2,1)}, u32[]{:S(2)}, u32[]{:S(2)}) collective-permute-start(bf16[512,1536]{1,0:T(8,128)(2,1)} %add_convert_fusion.1), channel_id=1, source_target_pairs={{0,2},{1,3},{2,0},{3,1},{4,6},{5,7},{6,4},{7,5},{8,10},{9,11},{10,... | collective-permute-start | bytes 4718600 | tf_op jit(solution)/shard_map/ppermute | solution.py:1195
  419.9 28.6 %collective-permute-start.32 = (bf16[2,256,1536]{2,1,0:T(8,128)(2,1)}, bf16[2,256,1536]{2,1,0:T(8,128)(2,1)}, u32[]{:S(2)}, u32[]{:S(2)}) collective-permute-start(bf16[2,256,1536]{2,1,0:T(8,128)(2,1)} %slice_bitcast_fusion.2), channel_id=1, source_target_pairs={{0,1},{1,0},{2,3},{3,2},{4,5},{5,4},{6,7},{7,6},{8,9},{9,8},{10,11... | collective-permute-start | bytes 4718600 | tf_op jit(solution)/shard_map/ppermute | solution.py:1191
  446.3 18.9 %collective-permute-start.34 = (bf16[2,256,1536]{2,1,0:T(8,128)(2,1)}, bf16[2,256,1536]{2,1,0:T(8,128)(2,1)}, u32[]{:S(2)}, u32[]{:S(2)}) collective-permute-start(bf16[2,256,1536]{2,1,0:T(8,128)(2,1)} %slice_bitcast_fusion), channel_id=1, source_target_pairs={{0,1},{1,0},{2,3},{3,2},{4,5},{5,4},{6,7},{7,6},{8,9},{9,8},{10,11... | collective-permute-start | bytes 4718600 | tf_op jit(solution)/shard_map/ppermute | solution.py:1191
  452.1 36.3 %collective-permute-start.35 = (bf16[2,256,1536]{2,1,0:T(8,128)(2,1)}, bf16[2,256,1536]{2,1,0:T(8,128)(2,1)}, u32[]{:S(2)}, u32[]{:S(2)}) collective-permute-start(bf16[2,256,1536]{2,1,0:T(8,128)(2,1)} %fusion.2), channel_id=1, source_target_pairs={{0,2},{1,3},{2,0},{3,1},{4,6},{5,7},{6,4},{7,5},{8,10},{9,11},{10,... | collective-permute-start | bytes 4718600 | tf_op jit(solution)/shard_map/ppermute | solution.py:1195
  461.3 35.3 %collective-permute-start.33 = (bf16[512,1536]{1,0:T(8,128)(2,1)}, bf16[512,1536]{1,0:T(8,128)(2,1)}, u32[]{:S(2)}, u32[]{:S(2)}) collective-permute-start(bf16[512,1536]{1,0:T(8,128)(2,1)} %sum_nt.14), channel_id=1, source_target_pairs={{0,1},{1,0},{2,3},{3,2},{4,5},{5,4},{6,7},{7,6},{8,9},{9,8},{10,11... | collective-permute-start | bytes 4718600 | tf_op jit(solution)/shard_map/ppermute | solution.py:1191
  (99 other events, 761.0 us)
Sparse Core Ops, SparseCore 0:
  12.3 60.4 all-gather.3
  75.6 78.7 all-gather.5
  157.1 77.9 all-gather.7
  238.6 94.3 reduce-scatter.3
  336.5 105.7 reduce-scatter.5
  445.1 38.2 reduce-scatter.7
